TPU v7x, 32 devices: a whole 2x2x4 slice. The times are simulated.
32 devices in a mesh: seq: 2 (over x), batch: 4 (over y, core), head: 4 (over z).
Axes of the slice: x: 2, y: 2, z: 4, core: 2. Of those that a mesh axis runs over, the one named last changes fastest.
Arguments:
- hidden: bfloat16 [4, 256, 16384], P('batch', None, 'seq'), may hold values from -760 to 760
- gain: float32 [16384], P('seq'), may hold values from 0.5 to 1.5
- key_weight: bfloat16 [16384, 1024], P('seq', 'head'), may hold values from -0.046875 to 0.046875
- value_weight: bfloat16 [16384, 1024], P('seq', 'head'), may hold values from -0.046875 to 0.046875
- positions: int32 [4, 256], P('batch', 'seq'), may hold values from 0 to 32767
- initial_basis: float32 [2048, 256], P('head'), may hold values from -6 to 6
Outputs:
- basis: float32 [2048, 256], P('head')
All inputs are finite; a program needn't handle non-finite values.
Results may differ from a plain program's by a relative error of at most 0.0063.
Values may be sent and summed in bfloat16 or wider, within the bound.
A program may use at most 64 MiB of HBM per device.

v0:
```python
import functools
import math

import jax
import jax.numpy as jnp
from jax import lax
from jax.experimental import pallas as pl
from jax.experimental.pallas import tpu as pltpu
from jax.sharding import PartitionSpec as P

D = 16384
HEAD_DIM = 128
ITERS = 4


EPSILON = 1e-05
ROTARY_BASE = 500000.0


def rotary(head_rows, position_row):
    half_width = head_rows.shape[-1] // 2
    index_row = jnp.arange(half_width, dtype=jnp.float32)
    frequency = jnp.exp(index_row * (-math.log(ROTARY_BASE) / half_width))
    angles = position_row.astype(jnp.float32)[:, None] * frequency[None, :]
    cosine = jnp.cos(angles)[:, None, :]
    sine_part = jnp.sin(angles)[:, None, :]
    first_half = head_rows[..., :half_width]
    second_half = head_rows[..., half_width:]
    return jnp.concatenate(
        [
            first_half * cosine - second_half * sine_part,
            second_half * cosine + first_half * sine_part,
        ],
        axis=-1,
    )


def whole_of(basis_block):
    return lax.all_gather(basis_block, "head", axis=0, tiled=True)


def total_squares(local_squares, local_tokens):
    all_squares = lax.psum(local_squares, "seq")
    return lax.dynamic_slice_in_dim(all_squares, lax.axis_index("seq") * local_tokens, local_tokens)


def gram_of(images):
    return lax.dot_general(
        images,
        images,
        (((0,), (0,)), ((), ())),
        precision=lax.Precision.HIGHEST,
        preferred_element_type=jnp.float32,
    )


def orthonormal(images, gram_matrix):
    factor = jnp.linalg.cholesky(gram_matrix)
    return lax.linalg.triangular_solve(
        factor, images, left_side=False, lower=True, transpose_a=True
    )


LANES = 128
SUBLANES = 8


def dot_of(left, right, left_axis, right_axis, precision=None):
    return lax.dot_general(
        left,
        right,
        (((left_axis,), (right_axis,)), ((), ())),
        precision=precision,
        preferred_element_type=jnp.float32,
    )


def exact(left, right, left_axis, right_axis):
    return dot_of(left, right, left_axis, right_axis, lax.Precision.HIGHEST)


def halves_of(value):
    high = value.astype(jnp.bfloat16)
    return high, (value - high.astype(jnp.float32)).astype(jnp.bfloat16)


def thrice(left, right, left_axis, right_axis):
    left_high, left_low = halves_of(left)
    right_high, right_low = halves_of(right)
    return (
        dot_of(left_high, right_high, left_axis, right_axis)
        + dot_of(left_high, right_low, left_axis, right_axis)
        + dot_of(left_low, right_high, left_axis, right_axis)
    )


def small_inverse(block):
    size = len(block)
    block = [list(line) for line in block]
    extra = [[None] * size for _ in range(size)]
    result = [[None] * size for _ in range(size)]

    def plus(left, right):
        return right if left is None else left if right is None else left + right

    def times(scale, value):
        return None if value is None else scale if isinstance(value, float) else scale * value

    def minus(left, right):
        return left if right is None else -right if left is None else left - right

    for i in range(size):
        extra[i][i] = 1.0
    for k in range(0, size, 2):
        first, cross, last = block[k][k], block[k + 1][k], block[k + 1][k + 1]
        scale = 1.0 / (first * last - cross * cross)
        for i in range(k + 2, size):
            one, two = block[i][k], block[i][k + 1]
            top = (one * last - two * cross) * scale
            low = (two * first - one * cross) * scale
            for j in range(k + 2, i + 1):
                block[i][j] = block[i][j] - (top * block[j][k] + low * block[j][k + 1])
            for j in range(k + 2):
                change = plus(times(top, extra[k][j]), times(low, extra[k + 1][j]))
                extra[i][j] = minus(extra[i][j], change)
        ratio = cross / first
        top_scale, low_scale = lax.rsqrt(first), lax.rsqrt(last - ratio * cross)
        for j in range(k + 2):
            result[k][j] = times(top_scale, extra[k][j])
            result[k + 1][j] = times(low_scale, minus(extra[k + 1][j], times(ratio, extra[k][j])))
    return result


def inverse_factor(matrix):
    size = matrix.shape[0]
    rows = lax.broadcasted_iota(jnp.int32, (SUBLANES, size), 0)
    lanes = lax.broadcasted_iota(jnp.int32, (SUBLANES, size), 1)
    groups = size // SUBLANES
    left = [matrix[SUBLANES * g : SUBLANES * (g + 1)] for g in range(groups)]
    right = [jnp.where(lanes == rows + SUBLANES * g, 1.0, 0.0) for g in range(groups)]

    def spread_row(value, at):
        return jnp.broadcast_to(value[at : at + 1, :], (SUBLANES, size))

    def spread_lane(value, at):
        return jnp.broadcast_to(value[:, at : at + 1], (SUBLANES, size))

    def stacked(values):
        total = jnp.zeros((SUBLANES, size), jnp.float32)
        for i, value in enumerate(values):
            if value is not None:
                total = jnp.where(rows == i, value, total)
        return total

    def combined(columns, value):
        terms = [columns[j] * spread_row(value, j) for j in range(SUBLANES)]
        while len(terms) > 1:
            terms = [terms[i] + terms[i + 1] for i in range(0, len(terms), 2)]
        return terms[0]

    for own in range(groups):
        pivot = own * SUBLANES
        tops = [spread_row(left[own], i) for i in range(SUBLANES)]
        block = [[spread_lane(tops[i], pivot + j) for j in range(i + 1)] for i in range(SUBLANES)]
        small = small_inverse(block)
        down = [stacked([small[i][j] for i in range(SUBLANES)]) for j in range(SUBLANES)]
        across = [stacked([small[j][i] for i in range(SUBLANES)]) for j in range(SUBLANES)]
        scaled_left, scaled_right = combined(down, left[own]), combined(down, right[own])
        right[own] = scaled_right
        if own + 1 == groups:
            break
        mixed_left, mixed_right = combined(across, scaled_left), combined(across, scaled_right)
        mixes = [
            (spread_row(mixed_left, j), spread_row(mixed_right, j)) for j in range(SUBLANES)
        ]
        for g in range(own + 1, groups):
            columns = [spread_lane(left[g], pivot + j) for j in range(SUBLANES)]
            for j in range(SUBLANES):
                left[g] = left[g] - columns[j] * mixes[j][0]
                right[g] = right[g] - columns[j] * mixes[j][1]
    return jnp.concatenate(right, axis=0)


def iterate_kernel(
    joint_ref, basis_ref, out_ref, high_ref, low_ref, rows_ref, gram_ref
):
    tokens, joint = joint_ref.shape
    rank = basis_ref.shape[1]
    panels = rank // LANES
    strip = 256
    for start in range(0, tokens, strip):
        kernel_rows = dot_of(joint_ref[start : start + strip, :], joint_ref[...], 1, 1) * (1.0 / tokens)
        high, low = halves_of(kernel_rows)
        high_ref[start : start + strip, :] = high
        low_ref[start : start + strip, :] = low
    basis_high, basis_low = halves_of(basis_ref[...])
    rows_ref[...] = dot_of(joint_ref[...], basis_high, 1, 0) + dot_of(joint_ref[...], basis_low, 1, 0)

    def step(iteration, carry):
        rows_high, rows_low = halves_of(rows_ref[...])
        images = (
            dot_of(high_ref[...], rows_high, 1, 0)
            + dot_of(high_ref[...], rows_low, 1, 0)
            + dot_of(low_ref[...], rows_high, 1, 0)
        )
        images_high, images_low = halves_of(images)
        gram_ref[...] = (
            dot_of(rows_high, images_high, 0, 0)
            + dot_of(rows_high, images_low, 0, 0)
            + dot_of(rows_low, images_high, 0, 0)
        ) * (1.0 / (tokens * joint))

        @pl.when(iteration < ITERS - 1)
        def _():
            rows_ref[...] = images

        for panel in range(panels):
            start, end = panel * LANES, (panel + 1) * LANES
            inverse = inverse_factor(gram_ref[start:end, start:end])
            columns = thrice(rows_ref[:, start:end], inverse, 1, 1)
            rows_ref[:, start:end] = columns
            if end < rank:
                scaled = exact(inverse, gram_ref[start:end, end:], 1, 0)
                gram_ref[end:, end:] -= exact(scaled, scaled, 0, 0)
                rows_ref[:, end:] -= thrice(columns, scaled, 1, 0)
        return carry

    lax.fori_loop(0, ITERS, step, 0)
    rows_high, rows_low = halves_of(rows_ref[...])
    width = out_ref.shape[0]
    own = joint_ref[:, pl.ds(pl.multiple_of(lax.axis_index("head") * width, width), width)]
    out_ref[...] = (dot_of(own, rows_high, 0, 0) + dot_of(own, rows_low, 0, 0)) * (1.0 / tokens)


def iterate(joint_all, basis_all):
    tokens, joint = joint_all.shape
    rank = basis_all.shape[1]
    return pl.pallas_call(
        iterate_kernel,
        out_shape=jax.ShapeDtypeStruct((joint // lax.axis_size("head"), rank), jnp.float32),
        in_specs=[pl.BlockSpec(memory_space=pltpu.VMEM)] * 2,
        out_specs=pl.BlockSpec(memory_space=pltpu.VMEM),
        scratch_shapes=[
            pltpu.VMEM((tokens, tokens), jnp.bfloat16),
            pltpu.VMEM((tokens, tokens), jnp.bfloat16),
            pltpu.VMEM((tokens, rank), jnp.float32),
            pltpu.VMEM((rank, rank), jnp.float32),
        ],
        compiler_params=pltpu.CompilerParams(vmem_limit_bytes=40 * 2**20),
    )(joint_all, basis_all)


def project_kernel(hidden_ref, gain_ref, key_ref, value_ref, partial_ref, squares_ref):
    key_columns = key_ref.shape[1]

    @pl.when(pl.program_id(0) == 0)
    def _():
        partial_ref[...] = jnp.zeros_like(partial_ref)
        squares_ref[...] = jnp.zeros_like(squares_ref)

    widened = hidden_ref[...].astype(jnp.float32)
    scaled = (widened * gain_ref[...]).astype(jnp.bfloat16)
    partial_ref[:, :key_columns] += dot_of(scaled, key_ref[...], 1, 0)
    partial_ref[:, key_columns:] += dot_of(scaled, value_ref[...], 1, 0)
    squared = widened * widened
    total = squares_ref[...]
    for start in range(0, squared.shape[1], LANES):
        total = total + squared[:, start : start + LANES]
    squares_ref[...] = total


def project(hidden_rows, gain, key_weight, value_weight):
    tokens, depth = hidden_rows.shape
    key_columns, value_columns = key_weight.shape[1], value_weight.shape[1]
    chunk = math.gcd(depth, 1024)
    return pl.pallas_call(
        project_kernel,
        grid=(depth // chunk,),
        out_shape=(
            jax.ShapeDtypeStruct((tokens, key_columns + value_columns), jnp.float32),
            jax.ShapeDtypeStruct((tokens, LANES), jnp.float32),
        ),
        in_specs=[
            pl.BlockSpec((tokens, chunk), lambda step: (0, step)),
            pl.BlockSpec((1, chunk), lambda step: (0, step)),
            pl.BlockSpec((chunk, key_columns), lambda step: (step, 0)),
            pl.BlockSpec((chunk, value_columns), lambda step: (step, 0)),
        ],
        out_specs=(
            pl.BlockSpec((tokens, key_columns + value_columns), lambda step: (0, 0)),
            pl.BlockSpec((tokens, LANES), lambda step: (0, 0)),
        ),
        compiler_params=pltpu.CompilerParams(
            dimension_semantics=("arbitrary",), vmem_limit_bytes=60 * 2**20
        ),
    )(hidden_rows, gain[None, :], key_weight, value_weight)


def gather_kernel(
    heads,
    partial_ref,
    squares_ref,
    cosine_ref,
    sine_ref,
    basis_ref,
    out_ref,
    whole_ref,
    peer_partial,
    peer_squares,
    swap_sems,
    z_sems,
    x_sems,
    y_sems,
    x_half_sems,
    y_half_sems,
    core_sems,
):
    x, b, z = lax.axis_index("seq"), lax.axis_index("batch"), lax.axis_index("head")
    local, width = peer_partial.shape
    half = width // 2
    rank = basis_ref.shape[1]
    piece = width // 8
    other_x, other_y = 1 - x, (b + 2) % 4
    partner = b + 1 - 2 * (b % 2)
    x_peer, y_peer, core_peer = (other_x, b, z), (x, other_y, z), (x, partner, z)

    def z_peer(d):
        return (x, b, (z + d) % heads)

    barrier = pltpu.get_barrier_semaphore()
    peers = [x_peer, y_peer, core_peer] + [z_peer(d) for d in range(1, heads)]
    for peer in peers:
        pl.semaphore_signal(barrier, inc=1, device_id=peer, device_id_type=pl.DeviceIdType.MESH)
    pl.semaphore_wait(barrier, len(peers))

    def copy(source, target, sems, peer):
        return pltpu.make_async_remote_copy(
            src_ref=source,
            dst_ref=target,
            send_sem=sems.at[0],
            recv_sem=sems.at[1],
            device_id=peer,
            device_id_type=pl.DeviceIdType.MESH,
        )

    def region(xs, bs, zs, start=0, size=width):
        row = pl.multiple_of((xs * 4 + bs) * local, local)
        column = pl.multiple_of(zs * width + start, half)
        return out_ref.at[pl.ds(row, local), pl.ds(column, size)]

    def piece_of(xs, bs, zs, start=0, size=rank):
        row = pl.multiple_of(zs * width + (xs * 4 + bs) * piece, piece)
        return whole_ref.at[pl.ds(row, piece), pl.ds(start, size)]

    started = []

    def send(area, sems, peer):
        going = copy(area, area, sems, peer)
        going.start()
        started.append(going)

    def arrive(area, sems, peer):
        copy(area, area, sems, peer).wait_recv()

    def source(d):
        return (z + heads - d) % heads

    order = [0] + sorted(range(1, heads), key=lambda d: (min(d, heads - d), d))
    own_piece = basis_ref.at[pl.ds(pl.multiple_of((x * 4 + b) * piece, piece), piece), :]
    for d in range(1, heads):
        going = copy(own_piece, piece_of(x, b, z), z_sems.at[1, d], z_peer(d))
        going.start()
        started.append(going)

    away = pl.ds(pl.multiple_of(other_x * local, local), local)
    mine = pl.ds(pl.multiple_of(x * local, local), local)
    swaps = [
        copy(partial_ref.at[away, :], peer_partial, swap_sems.at[0], x_peer),
        copy(squares_ref.at[away, :], peer_squares, swap_sems.at[1], x_peer),
    ]
    for swap in swaps:
        swap.start()
    whole_ref[pl.ds(pl.multiple_of(z * width, width), width), :] = basis_ref[...]
    for swap in swaps:
        swap.wait()
    squares = jnp.sum(squares_ref[mine, :] + peer_squares[...], axis=1, keepdims=True)
    projected = (partial_ref[mine, :] + peer_partial[...]) * lax.rsqrt(squares / D + EPSILON)
    row = pl.multiple_of((x * 4 + b) * local, local)
    for g in range(half // HEAD_DIM):
        key = projected[:, g * HEAD_DIM : (g + 1) * HEAD_DIM]
        turned = key * cosine_ref[...] + pltpu.roll(key, HEAD_DIM // 2, 1) * sine_ref[...]
        value = projected[:, half + g * HEAD_DIM : half + (g + 1) * HEAD_DIM]
        column = pl.multiple_of(z * width + 2 * g * HEAD_DIM, HEAD_DIM)
        out_ref[pl.ds(row, local), pl.ds(column, HEAD_DIM)] = turned.astype(jnp.bfloat16)
        column = pl.multiple_of(z * width + (2 * g + 1) * HEAD_DIM, HEAD_DIM)
        out_ref[pl.ds(row, local), pl.ds(column, HEAD_DIM)] = value.astype(jnp.bfloat16)

    for d in range(1, heads):
        send(region(x, b, z), z_sems.at[0, d], z_peer(d))

    def spread(kind, area, middle, d):
        mine = area(x, b, source(d))
        if d:
            arrive(mine, z_sems.at[kind, d], z_peer(d))
        send(mine, x_sems.at[kind, d], x_peer)
        send(mine, y_sems.at[kind, d], y_peer)
        send(mine, core_sems.at[kind, d, 0], core_peer)

    def relay(kind, area, middle, d):
        s = source(d)
        arrive(area(other_x, b, s), x_sems.at[kind, d], x_peer)
        send(area(other_x, b, s, middle, middle), y_half_sems.at[kind, d], y_peer)
        send(area(other_x, b, s), core_sems.at[kind, d, 1], core_peer)
        arrive(area(x, other_y, s), y_sems.at[kind, d], y_peer)
        send(area(x, other_y, s, 0, middle), x_half_sems.at[kind, d], x_peer)
        send(area(x, other_y, s), core_sems.at[kind, d, 2], core_peer)

    def finish(kind, area, middle, d):
        s = source(d)
        arrive(area(other_x, other_y, s, 0, middle), x_half_sems.at[kind, d], x_peer)
        arrive(area(other_x, other_y, s, middle, middle), y_half_sems.at[kind, d], y_peer)
        send(area(other_x, other_y, s), core_sems.at[kind, d, 3], core_peer)

    joint, pieces = (0, region, half), (1, piece_of, rank // 2)
    items = [joint + (0,)] + [pieces + (d,) for d in order[1:]] + [joint + (d,) for d in order[1:]]
    for turn in range(len(items) + 2):
        if turn < len(items):
            spread(*items[turn])
        if 1 <= turn < len(items) + 1:
            relay(*items[turn - 1])
        if turn >= 2:
            finish(*items[turn - 2])
    far = (partner + 2) % 4
    for kind, area, middle, d in items:
        s = source(d)
        places = [(x, partner), (other_x, partner), (x, far), (other_x, far)]
        for place, (xs, bs) in enumerate(places):
            arrive(area(xs, bs, s), core_sems.at[kind, d, place], core_peer)
    for going in started:
        going.wait_send()


def gather(partial, squares, positions, basis, heads, tokens):
    local, width = positions.shape[0], partial.shape[1]
    half_width = HEAD_DIM // 2
    frequency = jnp.exp(
        jnp.arange(half_width, dtype=jnp.float32) * (-math.log(ROTARY_BASE) / half_width)
    )
    angles = positions.astype(jnp.float32)[:, None] * frequency[None, :]
    cosine, sine = jnp.cos(angles), jnp.sin(angles)
    dma = pltpu.SemaphoreType.DMA
    return pl.pallas_call(
        functools.partial(gather_kernel, heads),
        out_shape=(
            jax.ShapeDtypeStruct((tokens, heads * width), jnp.bfloat16),
            jax.ShapeDtypeStruct((heads * width, basis.shape[1]), jnp.float32),
        ),
        in_specs=[pl.BlockSpec(memory_space=pltpu.VMEM)] * 5,
        out_specs=(pl.BlockSpec(memory_space=pltpu.VMEM),) * 2,
        scratch_shapes=[
            pltpu.VMEM((local, width), jnp.float32),
            pltpu.VMEM((local, LANES), jnp.float32),
            dma((2, 2)),
            dma((2, heads, 2)),
            dma((2, heads, 2)),
            dma((2, heads, 2)),
            dma((2, heads, 2)),
            dma((2, heads, 2)),
            dma((2, heads, 4, 2)),
        ],
        compiler_params=pltpu.CompilerParams(
            collective_id=0, has_side_effects=True, vmem_limit_bytes=24 * 2**20
        ),
    )(
        partial,
        squares,
        jnp.concatenate([cosine, cosine], axis=1),
        jnp.concatenate([-sine, sine], axis=1),
        basis,
    )


def body(hidden, gain, key_weight, value_weight, positions, initial_basis):
    hidden_rows = hidden[0]
    local_tokens = positions.shape[1]
    seqs, batches, heads = lax.axis_size("seq"), lax.axis_size("batch"), lax.axis_size("head")
    tokens = local_tokens * seqs * batches
    if seqs == 2 and batches == 4 and tokens <= initial_basis.shape[0] * heads:
        partial, squares = project(hidden_rows, gain, key_weight, value_weight)
        return iterate(*gather(partial, squares, positions[0], initial_basis, heads, tokens))
    widened = hidden_rows.astype(jnp.float32)
    scaled = (widened * gain).astype(jnp.bfloat16)
    local_squares = jnp.sum(widened * widened, axis=1)
    key_columns = key_weight.shape[1]
    weights = jnp.concatenate([key_weight, value_weight], axis=1)
    own_squares = total_squares(local_squares, local_tokens)
    projected = lax.psum_scatter(
        jnp.dot(scaled, weights, preferred_element_type=jnp.float32),
        "seq",
        scatter_dimension=0,
        tiled=True,
    )
    inverse_scale = lax.rsqrt(own_squares / D + EPSILON)
    projected = projected * inverse_scale[:, None]
    key_rows = rotary(projected[:, :key_columns].reshape(local_tokens, -1, HEAD_DIM), positions[0])
    value_rows = projected[:, key_columns:].reshape(local_tokens, -1, HEAD_DIM)
    joint_rows = (
        jnp.stack([key_rows, value_rows], axis=2).reshape(local_tokens, -1).astype(jnp.bfloat16)
    )
    partial_value = lax.dot_general(
        joint_rows,
        lax.all_gather(joint_rows, "head", axis=1, tiled=True),
        (((0,), (0,)), ((), ())),
        preferred_element_type=jnp.float32,
    )
    token_total = local_tokens * lax.axis_size("seq") * lax.axis_size("batch")
    basis_block = initial_basis
    covariance = lax.psum(partial_value, ("seq", "batch")) / token_total
    for iteration in range(ITERS):
        whole_basis = whole_of(basis_block)
        images = jnp.dot(
            covariance,
            whole_basis,
            precision=lax.Precision.HIGHEST,
            preferred_element_type=jnp.float32,
        )
        gram_matrix = lax.psum(gram_of(images), "head") / whole_basis.shape[0]
        basis_block = orthonormal(images, gram_matrix)
    return basis_block


def solution(mesh):
    return jax.shard_map(
        body,
        mesh=mesh,
        in_specs=(
            P("batch", None, "seq"),
            P("seq"),
            P("seq", "head"),
            P("seq", "head"),
            P("batch", "seq"),
            P("head", None),
        ),
        out_specs=P("head", None),
        check_vma=False,
    )
```

profile of v0, /device:TPU:0, one launch (start us, length us, event | category | flops | bytes accessed | tf_op | source)
XLA Modules:
  0.0 123.7 jit_solution(12964481932208982230)
XLA Ops:
  0.0 0.7 convert_bitcast_fusion
  0.7 0.3 fusion
  1.0 0.1 pad_maximum_fusion
  1.1 0.0 copy-start
  1.1 9.1 %shard_map.64 = (f32[256,512]{1,0:T(8,128)}, f32[256,128]{1,0:T(8,128)}) custom-call(bf16[256,8192]{1,0:T(8,128)(2,1)} %bitcast.4, f32[1,8192]{1,0:T(1,128)} %bitcast.5, bf16[8192,256]{1,0:T(8,128)(2,1)} %key_ref.1, bf16[8192,256]{1,0:T(8,128)(2,1)} %value_ref.1), custom_call_target="tpu_custom_call" | custom-call | tf_op jit(solution)/shard_map/pallas_call | solution.py:276
  10.2 0.0 copy-done
  10.2 0.0 copy-start.1
  10.2 1.0 copy-done.1
  11.2 0.0 copy-start.2
  11.2 0.9 copy-done.2
  12.1 43.2 %shard_map.65 = (bf16[1024,2048]{1,0:T(8,128)(2,1)S(1)}, f32[2048,256]{1,0:T(8,128)S(1)}) custom-call(f32[256,512]{1,0:T(8,128)S(1)} %copy-done.1, f32[256,128]{1,0:T(8,128)S(1)} %copy-done.2, f32[128,128]{1,0:T(8,128)S(1)} %get-tuple-element.16.cosine_ref, f32[128,128]{1,0:T(8,128)S(1)} %get-tuple-element.17.sine_ref, f32[512,256]{1,0:T(8,128)S(1)} %copy-done), custom_call_target="tpu_custom_call" | custom-call | tf_op jit(solution)/shard_map/pallas_call | solution.py:452
  55.4 68.3 %shard_map.66 = f32[512,256]{1,0:T(8,128)} custom-call(bf16[1024,2048]{1,0:T(8,128)(2,1)S(1)} %get-tuple-element.11.joint_ref, f32[2048,256]{1,0:T(8,128)S(1)} %get-tuple-element.12.basis_ref), custom_call_target="tpu_custom_call" | custom-call | tf_op jit(solution)/shard_map/pallas_call | solution.py:238
  (1 shorter events, 0.0 us)
Async XLA Ops:
  1.1 9.1 %copy-start = (f32[512,256]{1,0:T(8,128)S(1)}, f32[512,256]{1,0:T(8,128)}, u32[]{:S(2)}) copy-start(f32[512,256]{1,0:T(8,128)} %basis_ref.1) | copy-start | bytes 1572868
  10.2 1.0 copy-start.1
  11.2 0.9 copy-start.2
where the time goes:
time: 124 us
  Pallas kernels  121 us (98%)
  local copies, waits for them, and re-layouts  1.95 us (2%)
    pallas_call x1, Pallas kernels, iterate(): pl.pallas_call(iterate_kernel, out_shape=jax.ShapeDtypeStruct((joint // l...  68.3 us
    pallas_call x1, Pallas kernels, gather(): pl.pallas_call(functools.partial(gather_kernel, heads), out_shape=(jax.Sh...  43.2 us
    pallas_call x1, Pallas kernels, project(): pl.pallas_call(project_kernel, grid=(depth // chunk,), out_shape=(jax.Sha...  9.08 us

commit v1 on v0

--- a/solution.py
+++ b/solution.py
@@ -94,91 +94,91 @@
     )
 
 
-def small_inverse(block):
-    size = len(block)
-    block = [list(line) for line in block]
-    extra = [[None] * size for _ in range(size)]
-    result = [[None] * size for _ in range(size)]
-
-    def plus(left, right):
-        return right if left is None else left if right is None else left + right
-
-    def times(scale, value):
-        return None if value is None else scale if isinstance(value, float) else scale * value
-
-    def minus(left, right):
-        return left if right is None else -right if left is None else left - right
-
-    for i in range(size):
-        extra[i][i] = 1.0
-    for k in range(0, size, 2):
-        first, cross, last = block[k][k], block[k + 1][k], block[k + 1][k + 1]
-        scale = 1.0 / (first * last - cross * cross)
-        for i in range(k + 2, size):
-            one, two = block[i][k], block[i][k + 1]
+def inverse_factor(matrix):
+    size = matrix.shape[0]
+    shape = (SUBLANES, size)
+    rows = lax.broadcasted_iota(jnp.int32, shape, 0)
+    lanes = lax.broadcasted_iota(jnp.int32, shape, 1)
+    groups = size // SUBLANES
+    tiles = [matrix[SUBLANES * g : SUBLANES * (g + 1)] for g in range(groups)]
+    out = []
+
+    def row_of(value, at):
+        return jnp.broadcast_to(value[at : at + 1, :], shape)
+
+    def lane_of(value, at):
+        return jnp.broadcast_to(value[:, at : at + 1], shape)
+
+    def total(terms):
+        terms = list(terms)
+        while len(terms) > 1:
+            terms = [terms[i] + terms[i + 1] if i + 1 < len(terms) else terms[i] for i in range(0, len(terms), 2)]
+        return terms[0]
+
+    block = [lane_of(tiles[0], j) for j in range(SUBLANES)]
+    for own in range(groups):
+        pivot = own * SUBLANES
+        last_group = own + 1 == groups
+        if not last_group:
+            below = [lane_of(tiles[own + 1], pivot + j) for j in range(SUBLANES)]
+            after = [lane_of(tiles[own + 1], pivot + SUBLANES + j) for j in range(SUBLANES)]
+        factor = [None] * SUBLANES
+        turned, weighted = [], []
+        for k in range(0, SUBLANES, 2):
+            one, two = block[k], block[k + 1]
+            first, cross, last = row_of(one, k), row_of(two, k), row_of(two, k + 1)
+            scale = 1.0 / (first * last - cross * cross)
             top = (one * last - two * cross) * scale
             low = (two * first - one * cross) * scale
-            for j in range(k + 2, i + 1):
-                block[i][j] = block[i][j] - (top * block[j][k] + low * block[j][k + 1])
-            for j in range(k + 2):
-                change = plus(times(top, extra[k][j]), times(low, extra[k + 1][j]))
-                extra[i][j] = minus(extra[i][j], change)
-        ratio = cross / first
-        top_scale, low_scale = lax.rsqrt(first), lax.rsqrt(last - ratio * cross)
-        for j in range(k + 2):
-            result[k][j] = times(top_scale, extra[k][j])
-            result[k + 1][j] = times(low_scale, minus(extra[k + 1][j], times(ratio, extra[k][j])))
-    return result
-
-
-def inverse_factor(matrix):
-    size = matrix.shape[0]
-    rows = lax.broadcasted_iota(jnp.int32, (SUBLANES, size), 0)
-    lanes = lax.broadcasted_iota(jnp.int32, (SUBLANES, size), 1)
-    groups = size // SUBLANES
-    left = [matrix[SUBLANES * g : SUBLANES * (g + 1)] for g in range(groups)]
-    right = [jnp.where(lanes == rows + SUBLANES * g, 1.0, 0.0) for g in range(groups)]
-
-    def spread_row(value, at):
-        return jnp.broadcast_to(value[at : at + 1, :], (SUBLANES, size))
-
-    def spread_lane(value, at):
-        return jnp.broadcast_to(value[:, at : at + 1], (SUBLANES, size))
-
-    def stacked(values):
-        total = jnp.zeros((SUBLANES, size), jnp.float32)
-        for i, value in enumerate(values):
-            if value is not None:
-                total = jnp.where(rows == i, value, total)
-        return total
-
-    def combined(columns, value):
-        terms = [columns[j] * spread_row(value, j) for j in range(SUBLANES)]
-        while len(terms) > 1:
-            terms = [terms[i] + terms[i + 1] for i in range(0, len(terms), 2)]
-        return terms[0]
-
-    for own in range(groups):
-        pivot = own * SUBLANES
-        tops = [spread_row(left[own], i) for i in range(SUBLANES)]
-        block = [[spread_lane(tops[i], pivot + j) for j in range(i + 1)] for i in range(SUBLANES)]
-        small = small_inverse(block)
-        down = [stacked([small[i][j] for i in range(SUBLANES)]) for j in range(SUBLANES)]
-        across = [stacked([small[j][i] for i in range(SUBLANES)]) for j in range(SUBLANES)]
-        scaled_left, scaled_right = combined(down, left[own]), combined(down, right[own])
-        right[own] = scaled_right
-        if own + 1 == groups:
+            top_row, low_row = first * scale, last * scale
+            mixed = cross * scale
+            here, next_ = rows == k, rows == k + 1
+            pair = here | next_
+            top = jnp.where(here, -low_row, jnp.where(next_, mixed, top))
+            low = jnp.where(here, mixed, jnp.where(next_, -top_row, low))
+            heads = {}
+            for j in range(SUBLANES):
+                if j in (k, k + 1):
+                    continue
+                x, y = row_of(block[j], k), row_of(block[j], k + 1)
+                heads[j] = (x, y)
+                block[j] = jnp.where(pair, 0.0, block[j]) - (top * x + low * y)
+            block[k], block[k + 1] = -top, -low
+            ratio = cross / first
+            top_scale, low_scale = lax.rsqrt(first), lax.rsqrt(last - ratio * cross)
+            for j in range(k):
+                x, y = heads[j]
+                base = factor[j]
+                factor[j] = jnp.where(here, x * top_scale, jnp.where(next_, (y - ratio * x) * low_scale, base))
+            factor[k] = jnp.where(here, top_scale, jnp.where(next_, -ratio * low_scale, 0.0))
+            factor[k + 1] = jnp.where(next_, low_scale, 0.0)
+            if not last_group:
+                t1 = total([below[k]] + [heads[j][0] * below[j] for j in range(k)])
+                t2 = total([below[k + 1]] + [heads[j][1] * below[j] for j in range(k)])
+                turned += [t1, t2]
+                weighted += [(t1 * last - t2 * cross) * scale, (t2 * first - t1 * cross) * scale]
+        inside = (lanes >= pivot) & (lanes < pivot + SUBLANES)
+        held = jnp.where(inside, jnp.where(lanes == rows + pivot, 1.0, 0.0), tiles[own])
+        spread = [row_of(held, j) for j in range(SUBLANES)]
+        result = total([factor[j] * spread[j] for j in range(SUBLANES)])
+        out.append(jnp.where(lanes < pivot + SUBLANES, result, 0.0))
+        if last_group:
             break
-        mixed_left, mixed_right = combined(across, scaled_left), combined(across, scaled_right)
-        mixes = [
-            (spread_row(mixed_left, j), spread_row(mixed_right, j)) for j in range(SUBLANES)
+        mixed = total([block[j] * spread[j] for j in range(SUBLANES)])
+        mixes = [row_of(mixed, j) for j in range(SUBLANES)]
+        following = [
+            after[j] - total([turned[m] * row_of(weighted[m], j) for m in range(SUBLANES)])
+            for j in range(SUBLANES)
+        ]
+        columns = [
+            [below[j]] + [lane_of(tiles[g], pivot + j) for g in range(own + 2, groups)]
+            for j in range(SUBLANES)
         ]
         for g in range(own + 1, groups):
-            columns = [spread_lane(left[g], pivot + j) for j in range(SUBLANES)]
-            for j in range(SUBLANES):
-                left[g] = left[g] - columns[j] * mixes[j][0]
-                right[g] = right[g] - columns[j] * mixes[j][1]
-    return jnp.concatenate(right, axis=0)
+            changes = [columns[j][g - own - 1] * mixes[j] for j in range(SUBLANES)]
+            tiles[g] = jnp.where(inside, 0.0, tiles[g]) - total(changes)
+        block = following
+    return jnp.concatenate(out, axis=0)
 
 
 def iterate_kernel(

time: 124 us -> 105 us (0.85)
  Pallas kernels: 121 us -> 102 us
    pallas_call x1, Pallas kernels: 68.3 us -> 49.3 us  [iterate(): pl.pallas_call(iterate_kernel, out_shape=jax.ShapeDtypeStruct((joint // l...]
where the time goes in v1:
time: 105 us
  Pallas kernels  102 us (97%)
  local copies, waits for them, and re-layouts  1.95 us (2%)
  other arithmetic  1.08 us (1%)
    pallas_call x1, Pallas kernels, iterate(): pl.pallas_call(iterate_kernel, out_shape=jax.ShapeDtypeStruct((joint // l...  49.3 us
    pallas_call x1, Pallas kernels, gather(): pl.pallas_call(functools.partial(gather_kernel, heads), out_shape=(jax.Sh...  43.2 us
    pallas_call x1, Pallas kernels, project(): pl.pallas_call(project_kernel, grid=(depth // chunk,), out_shape=(jax.Sha...  9.08 us

profile of v1, /device:TPU:0, one launch (start us, length us, event | category | flops | bytes accessed | tf_op | source)
XLA Modules:
  0.0 104.7 jit_solution(6704746883381539444)
XLA Ops:
  0.0 0.7 convert_bitcast_fusion
  0.7 0.3 fusion
  1.0 0.1 pad_maximum_fusion
  1.1 0.0 copy-start
  1.1 9.1 %shard_map.64 = (f32[256,512]{1,0:T(8,128)}, f32[256,128]{1,0:T(8,128)}) custom-call(bf16[256,8192]{1,0:T(8,128)(2,1)} %bitcast.4, f32[1,8192]{1,0:T(1,128)} %bitcast.5, bf16[8192,256]{1,0:T(8,128)(2,1)} %key_ref.1, bf16[8192,256]{1,0:T(8,128)(2,1)} %value_ref.1), custom_call_target="tpu_custom_call" | custom-call | tf_op jit(solution)/shard_map/pallas_call | solution.py:276
  10.2 0.0 copy-done
  10.2 0.0 copy-start.1
  10.2 1.0 copy-done.1
  11.2 0.0 copy-start.2
  11.2 0.9 copy-done.2
  12.1 43.2 %shard_map.65 = (bf16[1024,2048]{1,0:T(8,128)(2,1)S(1)}, f32[2048,256]{1,0:T(8,128)S(1)}) custom-call(f32[256,512]{1,0:T(8,128)S(1)} %copy-done.1, f32[256,128]{1,0:T(8,128)S(1)} %copy-done.2, f32[128,128]{1,0:T(8,128)S(1)} %get-tuple-element.16.cosine_ref, f32[128,128]{1,0:T(8,128)S(1)} %get-tuple-element.17.sine_ref, f32[512,256]{1,0:T(8,128)S(1)} %copy-done), custom_call_target="tpu_custom_call" | custom-call | tf_op jit(solution)/shard_map/pallas_call | solution.py:452
  55.4 49.3 %shard_map.66 = f32[512,256]{1,0:T(8,128)} custom-call(bf16[1024,2048]{1,0:T(8,128)(2,1)S(1)} %get-tuple-element.11.joint_ref, f32[2048,256]{1,0:T(8,128)S(1)} %get-tuple-element.12.basis_ref), custom_call_target="tpu_custom_call" | custom-call | tf_op jit(solution)/shard_map/pallas_call | solution.py:238
  (1 shorter events, 0.0 us)
Async XLA Ops:
  1.1 9.1 %copy-start = (f32[512,256]{1,0:T(8,128)S(1)}, f32[512,256]{1,0:T(8,128)}, u32[]{:S(2)}) copy-start(f32[512,256]{1,0:T(8,128)} %basis_ref.1) | copy-start | bytes 1572868
  10.2 1.0 copy-start.1
  11.2 0.9 copy-start.2

commit v2 on v1

--- a/solution.py
+++ b/solution.py
@@ -250,63 +250,27 @@
     )(joint_all, basis_all)
 
 
-def project_kernel(hidden_ref, gain_ref, key_ref, value_ref, partial_ref, squares_ref):
-    key_columns = key_ref.shape[1]
-
-    @pl.when(pl.program_id(0) == 0)
-    def _():
-        partial_ref[...] = jnp.zeros_like(partial_ref)
-        squares_ref[...] = jnp.zeros_like(squares_ref)
-
-    widened = hidden_ref[...].astype(jnp.float32)
-    scaled = (widened * gain_ref[...]).astype(jnp.bfloat16)
-    partial_ref[:, :key_columns] += dot_of(scaled, key_ref[...], 1, 0)
-    partial_ref[:, key_columns:] += dot_of(scaled, value_ref[...], 1, 0)
-    squared = widened * widened
-    total = squares_ref[...]
-    for start in range(0, squared.shape[1], LANES):
-        total = total + squared[:, start : start + LANES]
-    squares_ref[...] = total
-
-
-def project(hidden_rows, gain, key_weight, value_weight):
-    tokens, depth = hidden_rows.shape
-    key_columns, value_columns = key_weight.shape[1], value_weight.shape[1]
-    chunk = math.gcd(depth, 1024)
-    return pl.pallas_call(
-        project_kernel,
-        grid=(depth // chunk,),
-        out_shape=(
-            jax.ShapeDtypeStruct((tokens, key_columns + value_columns), jnp.float32),
-            jax.ShapeDtypeStruct((tokens, LANES), jnp.float32),
-        ),
-        in_specs=[
-            pl.BlockSpec((tokens, chunk), lambda step: (0, step)),
-            pl.BlockSpec((1, chunk), lambda step: (0, step)),
-            pl.BlockSpec((chunk, key_columns), lambda step: (step, 0)),
-            pl.BlockSpec((chunk, value_columns), lambda step: (step, 0)),
-        ],
-        out_specs=(
-            pl.BlockSpec((tokens, key_columns + value_columns), lambda step: (0, 0)),
-            pl.BlockSpec((tokens, LANES), lambda step: (0, 0)),
-        ),
-        compiler_params=pltpu.CompilerParams(
-            dimension_semantics=("arbitrary",), vmem_limit_bytes=60 * 2**20
-        ),
-    )(hidden_rows, gain[None, :], key_weight, value_weight)
-
-
-def gather_kernel(
+def collect_kernel(
     heads,
-    partial_ref,
-    squares_ref,
+    hidden_ref,
+    gain_ref,
+    key_ref,
+    value_ref,
     cosine_ref,
     sine_ref,
     basis_ref,
     out_ref,
     whole_ref,
+    hidden_rows,
+    gain_row,
+    key_rows,
+    value_rows,
+    partial,
     peer_partial,
+    squares,
     peer_squares,
+    load_sems,
+    half_sems,
     swap_sems,
     z_sems,
     x_sems,
@@ -318,14 +282,51 @@
     x, b, z = lax.axis_index("seq"), lax.axis_index("batch"), lax.axis_index("head")
     local, width = peer_partial.shape
     half = width // 2
-    rank = basis_ref.shape[1]
+    rank = whole_ref.shape[1]
     piece = width // 8
+    depth = gain_row.shape[1]
+    chunks = load_sems.shape[1]
+    chunk = depth // chunks
     other_x, other_y = 1 - x, (b + 2) % 4
     partner = b + 1 - 2 * (b % 2)
     x_peer, y_peer, core_peer = (other_x, b, z), (x, other_y, z), (x, partner, z)
+    away = pl.ds(pl.multiple_of(other_x * local, local), local)
+    mine = pl.ds(pl.multiple_of(x * local, local), local)
 
     def z_peer(d):
         return (x, b, (z + d) % heads)
+
+    own_block = whole_ref.at[pl.ds(pl.multiple_of(z * width, width), width), :]
+    basis_load = pltpu.make_async_copy(basis_ref, own_block, half_sems.at[2, 0])
+    gain_load = pltpu.make_async_copy(gain_ref, gain_row, half_sems.at[2, 1])
+
+    def span(c):
+        return pl.ds(c * chunk, chunk)
+
+    def token_load(kind, area, c):
+        return pltpu.make_async_copy(
+            hidden_ref.at[area, span(c)], hidden_rows.at[area, span(c)], half_sems.at[kind, c]
+        )
+
+    away_loads = [token_load(0, away, c) for c in range(chunks)]
+    mine_loads = [token_load(1, mine, c) for c in range(chunks)]
+    key_loads = [
+        pltpu.make_async_copy(key_ref.at[span(c), :], key_rows.at[span(c), :], load_sems.at[0, c])
+        for c in range(chunks)
+    ]
+    value_loads = [
+        pltpu.make_async_copy(
+            value_ref.at[span(c), :], value_rows.at[span(c), :], load_sems.at[1, c]
+        )
+        for c in range(chunks)
+    ]
+    basis_load.start()
+    gain_load.start()
+    for c in range(chunks):
+        away_loads[c].start()
+        key_loads[c].start()
+    for load in value_loads + mine_loads:
+        load.start()
 
     barrier = pltpu.get_barrier_semaphore()
     peers = [x_peer, y_peer, core_peer] + [z_peer(d) for d in range(1, heads)]
@@ -365,46 +366,13 @@
     def source(d):
         return (z + heads - d) % heads
 
-    order = [0] + sorted(range(1, heads), key=lambda d: (min(d, heads - d), d))
-    own_piece = basis_ref.at[pl.ds(pl.multiple_of((x * 4 + b) * piece, piece), piece), :]
-    for d in range(1, heads):
-        going = copy(own_piece, piece_of(x, b, z), z_sems.at[1, d], z_peer(d))
-        going.start()
-        started.append(going)
-
-    away = pl.ds(pl.multiple_of(other_x * local, local), local)
-    mine = pl.ds(pl.multiple_of(x * local, local), local)
-    swaps = [
-        copy(partial_ref.at[away, :], peer_partial, swap_sems.at[0], x_peer),
-        copy(squares_ref.at[away, :], peer_squares, swap_sems.at[1], x_peer),
-    ]
-    for swap in swaps:
-        swap.start()
-    whole_ref[pl.ds(pl.multiple_of(z * width, width), width), :] = basis_ref[...]
-    for swap in swaps:
-        swap.wait()
-    squares = jnp.sum(squares_ref[mine, :] + peer_squares[...], axis=1, keepdims=True)
-    projected = (partial_ref[mine, :] + peer_partial[...]) * lax.rsqrt(squares / D + EPSILON)
-    row = pl.multiple_of((x * 4 + b) * local, local)
-    for g in range(half // HEAD_DIM):
-        key = projected[:, g * HEAD_DIM : (g + 1) * HEAD_DIM]
-        turned = key * cosine_ref[...] + pltpu.roll(key, HEAD_DIM // 2, 1) * sine_ref[...]
-        value = projected[:, half + g * HEAD_DIM : half + (g + 1) * HEAD_DIM]
-        column = pl.multiple_of(z * width + 2 * g * HEAD_DIM, HEAD_DIM)
-        out_ref[pl.ds(row, local), pl.ds(column, HEAD_DIM)] = turned.astype(jnp.bfloat16)
-        column = pl.multiple_of(z * width + (2 * g + 1) * HEAD_DIM, HEAD_DIM)
-        out_ref[pl.ds(row, local), pl.ds(column, HEAD_DIM)] = value.astype(jnp.bfloat16)
-
-    for d in range(1, heads):
-        send(region(x, b, z), z_sems.at[0, d], z_peer(d))
-
     def spread(kind, area, middle, d):
-        mine = area(x, b, source(d))
+        own = area(x, b, source(d))
         if d:
-            arrive(mine, z_sems.at[kind, d], z_peer(d))
-        send(mine, x_sems.at[kind, d], x_peer)
-        send(mine, y_sems.at[kind, d], y_peer)
-        send(mine, core_sems.at[kind, d, 0], core_peer)
+            arrive(own, z_sems.at[kind, d], z_peer(d))
+        send(own, x_sems.at[kind, d], x_peer)
+        send(own, y_sems.at[kind, d], y_peer)
+        send(own, core_sems.at[kind, d, 0], core_peer)
 
     def relay(kind, area, middle, d):
         s = source(d)
@@ -421,17 +389,98 @@
         arrive(area(other_x, other_y, s, middle, middle), y_half_sems.at[kind, d], y_peer)
         send(area(other_x, other_y, s), core_sems.at[kind, d, 3], core_peer)
 
-    joint, pieces = (0, region, half), (1, piece_of, rank // 2)
-    items = [joint + (0,)] + [pieces + (d,) for d in order[1:]] + [joint + (d,) for d in order[1:]]
-    for turn in range(len(items) + 2):
-        if turn < len(items):
-            spread(*items[turn])
-        if 1 <= turn < len(items) + 1:
-            relay(*items[turn - 1])
+    order = [0] + sorted(range(1, heads), key=lambda d: (min(d, heads - d), d))
+    joint = [(0, region, half, d) for d in order]
+    pieces = [(1, piece_of, rank // 2, d) for d in order[1:]]
+
+    basis_load.wait()
+    for d in order[1:]:
+        send(piece_of(x, b, z), z_sems.at[1, d], z_peer(d))
+
+    def prepare(area, c, total):
+        widened = hidden_rows[area, span(c)].astype(jnp.float32)
+        scaled = (widened * gain_row[:, span(c)]).astype(jnp.bfloat16)
+        hidden_rows[area, span(c)] = scaled
+        squared = widened * widened
+        for start in range(0, chunk, LANES):
+            total = total + squared[:, start : start + LANES]
+        return scaled, total
+
+    def across(total):
+        ones = jnp.ones((SUBLANES, LANES), jnp.float32)
+        return exact(ones, total, 1, 1)
+
+    def swap(source_ref, target_ref, index):
+        going = copy(source_ref, target_ref, swap_sems.at[index], x_peer)
+        going.start()
+        return going
+
+    gain_load.wait()
+    away_total = jnp.zeros((local, LANES), jnp.float32)
+    sums = jnp.zeros((local, half), jnp.float32)
+    for c in range(chunks):
+        away_loads[c].wait()
+        scaled, away_total = prepare(away, c, away_total)
+        key_loads[c].wait()
+        sums = sums + dot_of(scaled, key_rows[span(c), :], 1, 0)
+    partial[:, :half] = sums
+    squares[...] = across(away_total)
+    swaps = [
+        swap(squares, peer_squares, 0),
+        swap(partial.at[:, pl.ds(0, half)], peer_partial.at[:, pl.ds(0, half)], 1),
+    ]
+    for item in pieces:
+        spread(*item)
+    sums = jnp.zeros((local, half), jnp.float32)
+    for c in range(chunks):
+        value_loads[c].wait()
+        sums = sums + dot_of(hidden_rows[away, span(c)], value_rows[span(c), :], 1, 0)
+    partial[:, half:] = sums
+    swaps.append(swap(partial.at[:, pl.ds(half, half)], peer_partial.at[:, pl.ds(half, half)], 2))
+    for item in pieces:
+        relay(*item)
+    mine_total = jnp.zeros((local, LANES), jnp.float32)
+    key_sums = jnp.zeros((local, half), jnp.float32)
+    value_sums = jnp.zeros((local, half), jnp.float32)
+    for c in range(chunks):
+        mine_loads[c].wait()
+        scaled, mine_total = prepare(mine, c, mine_total)
+        key_sums = key_sums + dot_of(scaled, key_rows[span(c), :], 1, 0)
+        value_sums = value_sums + dot_of(scaled, value_rows[span(c), :], 1, 0)
+    own_squares = across(mine_total)
+    for item in pieces:
+        finish(*item)
+
+    swaps[0].wait()
+    eighths = jnp.full((SUBLANES, LANES), 1.0 / SUBLANES, jnp.float32)
+    inverse_scale = lax.rsqrt(exact(own_squares + peer_squares[...], eighths, 0, 0) / D + EPSILON)
+    row = pl.multiple_of((x * 4 + b) * local, local)
+    swaps[1].wait()
+    for g in range(half // HEAD_DIM):
+        spot = slice(g * HEAD_DIM, (g + 1) * HEAD_DIM)
+        key = (key_sums[:, spot] + peer_partial[:, spot]) * inverse_scale
+        turned = key * cosine_ref[...] + pltpu.roll(key, HEAD_DIM // 2, 1) * sine_ref[...]
+        column = pl.multiple_of(z * width + 2 * g * HEAD_DIM, HEAD_DIM)
+        out_ref[pl.ds(row, local), pl.ds(column, HEAD_DIM)] = turned.astype(jnp.bfloat16)
+    swaps[2].wait()
+    for g in range(half // HEAD_DIM):
+        spot = slice(g * HEAD_DIM, (g + 1) * HEAD_DIM)
+        there = slice(half + g * HEAD_DIM, half + (g + 1) * HEAD_DIM)
+        value = (value_sums[:, spot] + peer_partial[:, there]) * inverse_scale
+        column = pl.multiple_of(z * width + (2 * g + 1) * HEAD_DIM, HEAD_DIM)
+        out_ref[pl.ds(row, local), pl.ds(column, HEAD_DIM)] = value.astype(jnp.bfloat16)
+
+    for d in order[1:]:
+        send(region(x, b, z), z_sems.at[0, d], z_peer(d))
+    for turn in range(len(joint) + 2):
+        if turn < len(joint):
+            spread(*joint[turn])
+        if 1 <= turn < len(joint) + 1:
+            relay(*joint[turn - 1])
         if turn >= 2:
-            finish(*items[turn - 2])
+            finish(*joint[turn - 2])
     far = (partner + 2) % 4
-    for kind, area, middle, d in items:
+    for kind, area, middle, d in pieces + joint:
         s = source(d)
         places = [(x, partner), (other_x, partner), (x, far), (other_x, far)]
         for place, (xs, bs) in enumerate(places):
@@ -440,27 +489,40 @@
         going.wait_send()
 
 
-def gather(partial, squares, positions, basis, heads, tokens):
-    local, width = positions.shape[0], partial.shape[1]
+def collect(hidden_rows, gain, key_weight, value_weight, positions, basis, heads, tokens):
+    depth = hidden_rows.shape[1]
+    local = positions.shape[0]
+    half, width = key_weight.shape[1], key_weight.shape[1] + value_weight.shape[1]
     half_width = HEAD_DIM // 2
+    chunks = 4
     frequency = jnp.exp(
         jnp.arange(half_width, dtype=jnp.float32) * (-math.log(ROTARY_BASE) / half_width)
     )
     angles = positions.astype(jnp.float32)[:, None] * frequency[None, :]
     cosine, sine = jnp.cos(angles), jnp.sin(angles)
     dma = pltpu.SemaphoreType.DMA
+    anywhere = pl.BlockSpec(memory_space=pltpu.HBM)
+    inside = pl.BlockSpec(memory_space=pltpu.VMEM)
     return pl.pallas_call(
-        functools.partial(gather_kernel, heads),
+        functools.partial(collect_kernel, heads),
         out_shape=(
             jax.ShapeDtypeStruct((tokens, heads * width), jnp.bfloat16),
             jax.ShapeDtypeStruct((heads * width, basis.shape[1]), jnp.float32),
         ),
-        in_specs=[pl.BlockSpec(memory_space=pltpu.VMEM)] * 5,
-        out_specs=(pl.BlockSpec(memory_space=pltpu.VMEM),) * 2,
+        in_specs=[anywhere] * 4 + [inside] * 2 + [anywhere],
+        out_specs=(inside,) * 2,
         scratch_shapes=[
+            pltpu.VMEM(hidden_rows.shape, jnp.bfloat16),
+            pltpu.VMEM((1, depth), jnp.float32),
+            pltpu.VMEM(key_weight.shape, jnp.bfloat16),
+            pltpu.VMEM(value_weight.shape, jnp.bfloat16),
             pltpu.VMEM((local, width), jnp.float32),
-            pltpu.VMEM((local, LANES), jnp.float32),
-            dma((2, 2)),
+            pltpu.VMEM((local, width), jnp.float32),
+            pltpu.VMEM((SUBLANES, local), jnp.float32),
+            pltpu.VMEM((SUBLANES, local), jnp.float32),
+            dma((2, chunks)),
+            dma((3, chunks)),
+            dma((3, 2)),
             dma((2, heads, 2)),
             dma((2, heads, 2)),
             dma((2, heads, 2)),
@@ -469,11 +531,13 @@
             dma((2, heads, 4, 2)),
         ],
         compiler_params=pltpu.CompilerParams(
-            collective_id=0, has_side_effects=True, vmem_limit_bytes=24 * 2**20
+            collective_id=0, has_side_effects=True, vmem_limit_bytes=45 * 2**20
         ),
     )(
-        partial,
-        squares,
+        hidden_rows,
+        gain[None, :],
+        key_weight,
+        value_weight,
         jnp.concatenate([cosine, cosine], axis=1),
         jnp.concatenate([-sine, sine], axis=1),
         basis,
@@ -486,8 +550,18 @@
     seqs, batches, heads = lax.axis_size("seq"), lax.axis_size("batch"), lax.axis_size("head")
     tokens = local_tokens * seqs * batches
     if seqs == 2 and batches == 4 and tokens <= initial_basis.shape[0] * heads:
-        partial, squares = project(hidden_rows, gain, key_weight, value_weight)
-        return iterate(*gather(partial, squares, positions[0], initial_basis, heads, tokens))
+        return iterate(
+            *collect(
+                hidden_rows,
+                gain,
+                key_weight,
+                value_weight,
+                positions[0],
+                initial_basis,
+                heads,
+                tokens,
+            )
+        )
     widened = hidden_rows.astype(jnp.float32)
     scaled = (widened * gain).astype(jnp.bfloat16)
     local_squares = jnp.sum(widened * widened, axis=1)

time: 105 us -> 97.7 us (0.930)
  Pallas kernels: 102 us -> 94 us
    pallas_call x2 -> x1, Pallas kernels: 52.3 us -> 44.7 us  [collect(): pl.pallas_call(functools.partial(collect_kernel, heads), out_shape=(jax.S...]
where the time goes in v2:
time: 97.7 us; the launch traced here: 96.9 us
  Pallas kernels  94 us (96%)
  local copies, waits for them, and re-layouts  1.79 us (2%)
  other arithmetic  1.08 us (1%)
    pallas_call x1, Pallas kernels, iterate(): pl.pallas_call(iterate_kernel, out_shape=jax.ShapeDtypeStruct((joint // l...  49.3 us
    pallas_call x1, Pallas kernels, collect(): pl.pallas_call(functools.partial(collect_kernel, heads), out_shape=(jax.S...  44.7 us

profile of v2, /device:TPU:0, one launch (start us, length us, event | category | flops | bytes accessed | tf_op | source)
XLA Modules:
  0.0 96.9 jit_solution(5252496069135541618)
XLA Ops:
  0.0 0.7 convert_bitcast_fusion
  0.7 0.3 fusion
  1.0 0.1 pad_maximum_fusion
  1.1 0.0 copy-start
  1.1 1.0 %copy-done = f32[512,256]{1,0:T(8,128)S(1)} copy-done((f32[512,256]{1,0:T(8,128)S(1)}, f32[512,256]{1,0:T(8,128)}, u32[]{:S(2)}) %copy-start) | copy-done | bytes 524312
  2.1 0.0 copy-start.1
  2.1 0.8 copy-done.1
  2.9 44.7 %shard_map.64 = (bf16[1024,2048]{1,0:T(8,128)(2,1)S(1)}, f32[2048,256]{1,0:T(8,128)S(1)}) custom-call(bf16[256,8192]{1,0:T(8,128)(2,1)} %bitcast.5, f32[1,8192]{1,0:T(1,128)S(1)} %bitcast.4, bf16[8192,256]{1,0:T(8,128)(2,1)} %key_ref.1, bf16[8192,256]{1,0:T(8,128)(2,1)} %value_ref.1, f32[128,128]{1,0:T(8,128)S(1)} %get-tuple-element.12.cosine_ref, ...), custom_call_target="tpu_custom_call" | custom-call | tf_op jit(solution)/shard_map/pallas_call | solution.py:506
  47.6 49.3 %shard_map.65 = f32[512,256]{1,0:T(8,128)} custom-call(bf16[1024,2048]{1,0:T(8,128)(2,1)S(1)} %get-tuple-element.7.joint_ref, f32[2048,256]{1,0:T(8,128)S(1)} %get-tuple-element.8.basis_ref), custom_call_target="tpu_custom_call" | custom-call | tf_op jit(solution)/shard_map/pallas_call | solution.py:238
  (1 shorter events, 0.0 us)
Async XLA Ops:
  1.1 1.0 %copy-start = (f32[512,256]{1,0:T(8,128)S(1)}, f32[512,256]{1,0:T(8,128)}, u32[]{:S(2)}) copy-start(f32[512,256]{1,0:T(8,128)} %basis_ref.1) | copy-start | bytes 1572868
  2.1 0.8 copy-start.1

commit v3 on v2

--- a/solution.py
+++ b/solution.py
@@ -181,20 +181,10 @@
     return jnp.concatenate(out, axis=0)
 
 
-def iterate_kernel(
-    joint_ref, basis_ref, out_ref, high_ref, low_ref, rows_ref, gram_ref
-):
-    tokens, joint = joint_ref.shape
-    rank = basis_ref.shape[1]
+def iterate_kernel(high_ref, low_ref, start_ref, own_ref, out_ref, rows_ref, gram_ref, joint):
+    tokens, rank = start_ref.shape
     panels = rank // LANES
-    strip = 256
-    for start in range(0, tokens, strip):
-        kernel_rows = dot_of(joint_ref[start : start + strip, :], joint_ref[...], 1, 1) * (1.0 / tokens)
-        high, low = halves_of(kernel_rows)
-        high_ref[start : start + strip, :] = high
-        low_ref[start : start + strip, :] = low
-    basis_high, basis_low = halves_of(basis_ref[...])
-    rows_ref[...] = dot_of(joint_ref[...], basis_high, 1, 0) + dot_of(joint_ref[...], basis_low, 1, 0)
+    rows_ref[...] = start_ref[...]
 
     def step(iteration, carry):
         rows_high, rows_low = halves_of(rows_ref[...])
@@ -227,27 +217,27 @@
 
     lax.fori_loop(0, ITERS, step, 0)
     rows_high, rows_low = halves_of(rows_ref[...])
-    width = out_ref.shape[0]
-    own = joint_ref[:, pl.ds(pl.multiple_of(lax.axis_index("head") * width, width), width)]
+    own = own_ref[...]
     out_ref[...] = (dot_of(own, rows_high, 0, 0) + dot_of(own, rows_low, 0, 0)) * (1.0 / tokens)
 
 
-def iterate(joint_all, basis_all):
-    tokens, joint = joint_all.shape
-    rank = basis_all.shape[1]
+def iterate(high, low, start, own, joint):
+    tokens, rank = start.shape
+
+    def kernel(*refs):
+        iterate_kernel(*refs, joint)
+
     return pl.pallas_call(
-        iterate_kernel,
-        out_shape=jax.ShapeDtypeStruct((joint // lax.axis_size("head"), rank), jnp.float32),
-        in_specs=[pl.BlockSpec(memory_space=pltpu.VMEM)] * 2,
+        kernel,
+        out_shape=jax.ShapeDtypeStruct((own.shape[1], rank), jnp.float32),
+        in_specs=[pl.BlockSpec(memory_space=pltpu.VMEM)] * 4,
         out_specs=pl.BlockSpec(memory_space=pltpu.VMEM),
         scratch_shapes=[
-            pltpu.VMEM((tokens, tokens), jnp.bfloat16),
-            pltpu.VMEM((tokens, tokens), jnp.bfloat16),
             pltpu.VMEM((tokens, rank), jnp.float32),
             pltpu.VMEM((rank, rank), jnp.float32),
         ],
         compiler_params=pltpu.CompilerParams(vmem_limit_bytes=40 * 2**20),
-    )(joint_all, basis_all)
+    )(high, low, start, own)
 
 
 def collect_kernel(
@@ -259,8 +249,13 @@
     cosine_ref,
     sine_ref,
     basis_ref,
+    high_ref,
+    low_ref,
+    rows_ref,
+    own_ref,
     out_ref,
     whole_ref,
+    token_sums,
     hidden_rows,
     gain_row,
     key_rows,
@@ -293,8 +288,18 @@
     away = pl.ds(pl.multiple_of(other_x * local, local), local)
     mine = pl.ds(pl.multiple_of(x * local, local), local)
 
-    def z_peer(d):
-        return (x, b, (z + d) % heads)
+    def nearest(turn):
+        if turn == 0 or heads != 4:
+            return (z + turn) % heads
+        side = z // 2
+        inner = z + side * (3 - 2 * z)
+        place = (1 + inner, 2 - 2 * inner, 3)[turn - 1]
+        return 3 * side + (1 - 2 * side) * place
+
+    sources = [nearest(turn) for turn in range(heads)]
+
+    def z_peer(turn):
+        return (x, b, sources[turn])
 
     own_block = whole_ref.at[pl.ds(pl.multiple_of(z * width, width), width), :]
     basis_load = pltpu.make_async_copy(basis_ref, own_block, half_sems.at[2, 0])
@@ -363,39 +368,82 @@
     def arrive(area, sems, peer):
         copy(area, area, sems, peer).wait_recv()
 
-    def source(d):
-        return (z + heads - d) % heads
-
-    def spread(kind, area, middle, d):
-        own = area(x, b, source(d))
-        if d:
-            arrive(own, z_sems.at[kind, d], z_peer(d))
-        send(own, x_sems.at[kind, d], x_peer)
-        send(own, y_sems.at[kind, d], y_peer)
-        send(own, core_sems.at[kind, d, 0], core_peer)
-
-    def relay(kind, area, middle, d):
-        s = source(d)
-        arrive(area(other_x, b, s), x_sems.at[kind, d], x_peer)
-        send(area(other_x, b, s, middle, middle), y_half_sems.at[kind, d], y_peer)
-        send(area(other_x, b, s), core_sems.at[kind, d, 1], core_peer)
-        arrive(area(x, other_y, s), y_sems.at[kind, d], y_peer)
-        send(area(x, other_y, s, 0, middle), x_half_sems.at[kind, d], x_peer)
-        send(area(x, other_y, s), core_sems.at[kind, d, 2], core_peer)
-
-    def finish(kind, area, middle, d):
-        s = source(d)
-        arrive(area(other_x, other_y, s, 0, middle), x_half_sems.at[kind, d], x_peer)
-        arrive(area(other_x, other_y, s, middle, middle), y_half_sems.at[kind, d], y_peer)
-        send(area(other_x, other_y, s), core_sems.at[kind, d, 3], core_peer)
-
-    order = [0] + sorted(range(1, heads), key=lambda d: (min(d, heads - d), d))
-    joint = [(0, region, half, d) for d in order]
-    pieces = [(1, piece_of, rank // 2, d) for d in order[1:]]
+    def send_z(area, kind, turn):
+        going = pltpu.make_async_remote_copy(
+            src_ref=area,
+            dst_ref=area,
+            send_sem=z_sems.at[kind, sources[turn], 0],
+            recv_sem=z_sems.at[kind, z, 1],
+            device_id=z_peer(turn),
+            device_id_type=pl.DeviceIdType.MESH,
+        )
+        going.start()
+        started.append(going)
+
+    def spread(kind, area, middle, turn):
+        s = sources[turn]
+        own = area(x, b, s)
+        if turn:
+            arrive(own, z_sems.at[kind, s], z_peer(turn))
+        send(own, x_sems.at[kind, turn], x_peer)
+        send(own, y_sems.at[kind, turn], y_peer)
+        send(own, core_sems.at[kind, turn, 0], core_peer)
+
+    def relay(kind, area, middle, turn):
+        s = sources[turn]
+        arrive(area(other_x, b, s), x_sems.at[kind, turn], x_peer)
+        beyond = area(other_x, b, s, middle, middle) if middle else area(other_x, b, s)
+        send(beyond, y_half_sems.at[kind, turn], y_peer)
+        send(area(other_x, b, s), core_sems.at[kind, turn, 1], core_peer)
+        arrive(area(x, other_y, s), y_sems.at[kind, turn], y_peer)
+        if middle:
+            send(area(x, other_y, s, 0, middle), x_half_sems.at[kind, turn], x_peer)
+        send(area(x, other_y, s), core_sems.at[kind, turn, 2], core_peer)
+
+    def finish(kind, area, middle, turn):
+        s = sources[turn]
+        if middle:
+            arrive(area(other_x, other_y, s, 0, middle), x_half_sems.at[kind, turn], x_peer)
+        beyond = area(other_x, other_y, s, middle, middle) if middle else area(other_x, other_y, s)
+        arrive(beyond, y_half_sems.at[kind, turn], y_peer)
+        send(area(other_x, other_y, s), core_sems.at[kind, turn, 3], core_peer)
+
+    far = (partner + 2) % 4
+
+    def gathered(kind, area, middle, turn):
+        places = [(x, partner), (other_x, partner), (x, far), (other_x, far)]
+        for place, (xs, bs) in enumerate(places):
+            arrive(area(xs, bs, sources[turn]), core_sems.at[kind, turn, place], core_peer)
+
+    joint = [(0, region, half, turn) for turn in range(heads)]
+    pieces = [(1, piece_of, 0, turn) for turn in range(1, heads)]
+    tokens, strip = out_ref.shape[0], 256
+
+    def accumulate(turn):
+        place = pl.multiple_of(sources[turn] * width, width)
+        block = out_ref[:, pl.ds(place, width)]
+        basis_high, basis_low = halves_of(whole_ref[pl.ds(place, width), :])
+        for start in range(0, tokens, strip):
+            area = slice(start, start + strip)
+            part = out_ref[area, pl.ds(place, width)]
+            product = dot_of(part, block, 1, 1)
+            rows = dot_of(part, basis_high, 1, 0) + dot_of(part, basis_low, 1, 0)
+            if turn:
+                product = product + token_sums[area, :]
+                rows = rows + rows_ref[area, :]
+            rows_ref[area, :] = rows
+            if turn < heads - 1:
+                token_sums[area, :] = product
+            else:
+                high, low = halves_of(product * (1.0 / tokens))
+                high_ref[area, :] = high
+                low_ref[area, :] = low
+            if turn == 0:
+                own_ref[area, :] = part
 
     basis_load.wait()
-    for d in order[1:]:
-        send(piece_of(x, b, z), z_sems.at[1, d], z_peer(d))
+    for turn in range(1, heads):
+        send_z(piece_of(x, b, z), 1, turn)
 
     def prepare(area, c, total):
         widened = hidden_rows[area, span(c)].astype(jnp.float32)
@@ -470,21 +518,21 @@
         column = pl.multiple_of(z * width + (2 * g + 1) * HEAD_DIM, HEAD_DIM)
         out_ref[pl.ds(row, local), pl.ds(column, HEAD_DIM)] = value.astype(jnp.bfloat16)
 
-    for d in order[1:]:
-        send(region(x, b, z), z_sems.at[0, d], z_peer(d))
-    for turn in range(len(joint) + 2):
+    for turn in range(1, heads):
+        send_z(region(x, b, z), 0, turn)
+    for turn in range(len(joint) + 3):
         if turn < len(joint):
             spread(*joint[turn])
         if 1 <= turn < len(joint) + 1:
             relay(*joint[turn - 1])
-        if turn >= 2:
+        if 2 <= turn < len(joint) + 2:
             finish(*joint[turn - 2])
-    far = (partner + 2) % 4
-    for kind, area, middle, d in pieces + joint:
-        s = source(d)
-        places = [(x, partner), (other_x, partner), (x, far), (other_x, far)]
-        for place, (xs, bs) in enumerate(places):
-            arrive(area(xs, bs, s), core_sems.at[kind, d, place], core_peer)
+        if turn == 2:
+            for item in pieces:
+                gathered(*item)
+        if turn >= 3:
+            gathered(*joint[turn - 3])
+            accumulate(turn - 3)
     for going in started:
         going.wait_send()
 
@@ -506,12 +554,17 @@
     return pl.pallas_call(
         functools.partial(collect_kernel, heads),
         out_shape=(
-            jax.ShapeDtypeStruct((tokens, heads * width), jnp.bfloat16),
-            jax.ShapeDtypeStruct((heads * width, basis.shape[1]), jnp.float32),
+            jax.ShapeDtypeStruct((tokens, tokens), jnp.bfloat16),
+            jax.ShapeDtypeStruct((tokens, tokens), jnp.bfloat16),
+            jax.ShapeDtypeStruct((tokens, basis.shape[1]), jnp.float32),
+            jax.ShapeDtypeStruct((tokens, width), jnp.bfloat16),
         ),
         in_specs=[anywhere] * 4 + [inside] * 2 + [anywhere],
-        out_specs=(inside,) * 2,
+        out_specs=(inside,) * 4,
         scratch_shapes=[
+            pltpu.VMEM((tokens, heads * width), jnp.bfloat16),
+            pltpu.VMEM((heads * width, basis.shape[1]), jnp.float32),
+            pltpu.VMEM((tokens, tokens), jnp.float32),
             pltpu.VMEM(hidden_rows.shape, jnp.bfloat16),
             pltpu.VMEM((1, depth), jnp.float32),
             pltpu.VMEM(key_weight.shape, jnp.bfloat16),
@@ -550,18 +603,17 @@
     seqs, batches, heads = lax.axis_size("seq"), lax.axis_size("batch"), lax.axis_size("head")
     tokens = local_tokens * seqs * batches
     if seqs == 2 and batches == 4 and tokens <= initial_basis.shape[0] * heads:
-        return iterate(
-            *collect(
-                hidden_rows,
-                gain,
-                key_weight,
-                value_weight,
-                positions[0],
-                initial_basis,
-                heads,
-                tokens,
-            )
+        collected = collect(
+            hidden_rows,
+            gain,
+            key_weight,
+            value_weight,
+            positions[0],
+            initial_basis,
+            heads,
+            tokens,
         )
+        return iterate(*collected, initial_basis.shape[0] * heads)
     widened = hidden_rows.astype(jnp.float32)
     scaled = (widened * gain).astype(jnp.bfloat16)
     local_squares = jnp.sum(widened * widened, axis=1)

time: 97.7 us -> 93.7 us (0.959)
  Pallas kernels: 94 us -> 90.5 us
    pallas_call x1, Pallas kernels: 49.3 us -> 42.4 us  [iterate(): pl.pallas_call(kernel, out_shape=jax.ShapeDtypeStruct((own.shape[1], rank...]
    pallas_call x1, Pallas kernels: 44.7 us -> 48.1 us  [collect(): pl.pallas_call(functools.partial(collect_kernel, heads), out_shape=(jax.S...]
where the time goes in v3:
time: 93.7 us; the launch traced here: 93.4 us
  Pallas kernels  90.5 us (97%)
  local copies, waits for them, and re-layouts  1.79 us (2%)
  other arithmetic  1.08 us (1%)
    pallas_call x1, Pallas kernels, collect(): pl.pallas_call(functools.partial(collect_kernel, heads), out_shape=(jax.S...  48.1 us
    pallas_call x1, Pallas kernels, iterate(): pl.pallas_call(kernel, out_shape=jax.ShapeDtypeStruct((own.shape[1], rank...  42.4 us

profile of v3, /device:TPU:0, one launch (start us, length us, event | category | flops | bytes accessed | tf_op | source)
XLA Modules:
  0.0 93.4 jit_solution(11312246385711094287)
XLA Ops:
  0.0 0.7 convert_bitcast_fusion
  0.7 0.3 fusion
  1.0 0.1 pad_maximum_fusion
  1.1 0.0 copy-start
  1.1 1.0 %copy-done = f32[512,256]{1,0:T(8,128)S(1)} copy-done((f32[512,256]{1,0:T(8,128)S(1)}, f32[512,256]{1,0:T(8,128)}, u32[]{:S(2)}) %copy-start) | copy-done | bytes 524312
  2.1 0.0 copy-start.1
  2.1 0.8 copy-done.1
  2.9 48.1 %shard_map.64 = (bf16[1024,1024]{1,0:T(8,128)(2,1)S(1)}, bf16[1024,1024]{1,0:T(8,128)(2,1)S(1)}, f32[1024,256]{1,0:T(8,128)S(1)}, bf16[1024,512]{1,0:T(8,128)(2,1)S(1)}) custom-call(bf16[256,8192]{1,0:T(8,128)(2,1)} %bitcast.5, f32[1,8192]{1,0:T(1,128)S(1)} %bitcast.4, bf16[8192,256]{1,0:T(8,128)(2,1)} %key_ref.1, bf16[8192,256]{1,0:T(8,128)(2,1)} %value_ref.1, ...), custom_call_target="tpu_custom_call" | custom-call | tf_op jit(solution)/shard_map/pallas_call | solution.py:554
  51.0 42.4 %shard_map.65 = f32[512,256]{1,0:T(8,128)} custom-call(bf16[1024,1024]{1,0:T(8,128)(2,1)S(1)} %get-tuple-element.9.refs_0_, bf16[1024,1024]{1,0:T(8,128)(2,1)S(1)} %get-tuple-element.10.refs_1_, f32[1024,256]{1,0:T(8,128)S(1)} %get-tuple-element.11.refs_2_, bf16[1024,512]{1,0:T(8,128)(2,1)S(1)} %get-tuple-element.12.refs_3_), custom_call_target="tpu_custom_call" | custom-call | tf_op jit(solution)/shard_map/pallas_call | solution.py:230
  (1 shorter events, 0.0 us)
Async XLA Ops:
  1.1 1.0 %copy-start = (f32[512,256]{1,0:T(8,128)S(1)}, f32[512,256]{1,0:T(8,128)}, u32[]{:S(2)}) copy-start(f32[512,256]{1,0:T(8,128)} %basis_ref.1) | copy-start | bytes 1572868
  2.1 0.8 copy-start.1

commit v4 on v3

--- a/solution.py
+++ b/solution.py
@@ -63,6 +63,7 @@
 
 LANES = 128
 SUBLANES = 8
+AHEAD = True
 
 
 def dot_of(left, right, left_axis, right_axis, precision=None):
@@ -110,32 +111,38 @@
         return jnp.broadcast_to(value[:, at : at + 1], shape)
 
     def total(terms):
-        terms = list(terms)
         while len(terms) > 1:
-            terms = [terms[i] + terms[i + 1] if i + 1 < len(terms) else terms[i] for i in range(0, len(terms), 2)]
+            pairs = [terms[i] + terms[i + 1] for i in range(0, len(terms) - 1, 2)]
+            terms = pairs + terms[2 * len(pairs) :]
         return terms[0]
 
-    block = [lane_of(tiles[0], j) for j in range(SUBLANES)]
+    zero = jnp.zeros(shape, jnp.float32)
     for own in range(groups):
         pivot = own * SUBLANES
+        block = [lane_of(tiles[own], pivot + j) for j in range(SUBLANES)]
+        if AHEAD and own:
+            block = following
         last_group = own + 1 == groups
         if not last_group:
             below = [lane_of(tiles[own + 1], pivot + j) for j in range(SUBLANES)]
-            after = [lane_of(tiles[own + 1], pivot + SUBLANES + j) for j in range(SUBLANES)]
+            if AHEAD:
+                after = [lane_of(tiles[own + 1], pivot + SUBLANES + j) for j in range(SUBLANES)]
         factor = [None] * SUBLANES
         turned, weighted = [], []
         for k in range(0, SUBLANES, 2):
             one, two = block[k], block[k + 1]
+            if not AHEAD:
+                one, two = one + zero, two + zero
             first, cross, last = row_of(one, k), row_of(two, k), row_of(two, k + 1)
             scale = 1.0 / (first * last - cross * cross)
-            top = (one * last - two * cross) * scale
-            low = (two * first - one * cross) * scale
-            top_row, low_row = first * scale, last * scale
             mixed = cross * scale
             here, next_ = rows == k, rows == k + 1
             pair = here | next_
-            top = jnp.where(here, -low_row, jnp.where(next_, mixed, top))
-            low = jnp.where(here, mixed, jnp.where(next_, -top_row, low))
+            first_scaled, last_scaled = first * scale, last * scale
+            top = one * last_scaled - two * mixed
+            low = two * first_scaled - one * mixed
+            top = jnp.where(here, -last_scaled, jnp.where(next_, mixed, top))
+            low = jnp.where(here, mixed, jnp.where(next_, -first_scaled, low))
             heads = {}
             for j in range(SUBLANES):
                 if j in (k, k + 1):
@@ -146,17 +153,18 @@
             block[k], block[k + 1] = -top, -low
             ratio = cross / first
             top_scale, low_scale = lax.rsqrt(first), lax.rsqrt(last - ratio * cross)
+            ratio_scale = ratio * low_scale
             for j in range(k):
                 x, y = heads[j]
-                base = factor[j]
-                factor[j] = jnp.where(here, x * top_scale, jnp.where(next_, (y - ratio * x) * low_scale, base))
-            factor[k] = jnp.where(here, top_scale, jnp.where(next_, -ratio * low_scale, 0.0))
+                lower = y * low_scale - x * ratio_scale
+                factor[j] = jnp.where(here, x * top_scale, jnp.where(next_, lower, factor[j]))
+            factor[k] = jnp.where(here, top_scale, jnp.where(next_, -ratio_scale, 0.0))
             factor[k + 1] = jnp.where(next_, low_scale, 0.0)
-            if not last_group:
+            if AHEAD and not last_group:
                 t1 = total([below[k]] + [heads[j][0] * below[j] for j in range(k)])
                 t2 = total([below[k + 1]] + [heads[j][1] * below[j] for j in range(k)])
                 turned += [t1, t2]
-                weighted += [(t1 * last - t2 * cross) * scale, (t2 * first - t1 * cross) * scale]
+                weighted += [t1 * last_scaled - t2 * mixed, t2 * first_scaled - t1 * mixed]
         inside = (lanes >= pivot) & (lanes < pivot + SUBLANES)
         held = jnp.where(inside, jnp.where(lanes == rows + pivot, 1.0, 0.0), tiles[own])
         spread = [row_of(held, j) for j in range(SUBLANES)]
@@ -166,10 +174,11 @@
             break
         mixed = total([block[j] * spread[j] for j in range(SUBLANES)])
         mixes = [row_of(mixed, j) for j in range(SUBLANES)]
-        following = [
-            after[j] - total([turned[m] * row_of(weighted[m], j) for m in range(SUBLANES)])
-            for j in range(SUBLANES)
-        ]
+        if AHEAD:
+            following = [
+                after[j] - total([turned[m] * row_of(weighted[m], j) for m in range(SUBLANES)])
+                for j in range(SUBLANES)
+            ]
         columns = [
             [below[j]] + [lane_of(tiles[g], pivot + j) for g in range(own + 2, groups)]
             for j in range(SUBLANES)
@@ -177,52 +186,77 @@
         for g in range(own + 1, groups):
             changes = [columns[j][g - own - 1] * mixes[j] for j in range(SUBLANES)]
             tiles[g] = jnp.where(inside, 0.0, tiles[g]) - total(changes)
-        block = following
-    return jnp.concatenate(out, axis=0)
-
-
-def iterate_kernel(high_ref, low_ref, start_ref, own_ref, out_ref, rows_ref, gram_ref, joint):
-    tokens, rank = start_ref.shape
-    panels = rank // LANES
-    rows_ref[...] = start_ref[...]
+        yield
+    yield jnp.concatenate(out, axis=0)
+
+
+def factors_of(*matrices):
+    running = [inverse_factor(matrix) for matrix in matrices]
+    for _ in range(matrices[0].shape[0] // SUBLANES):
+        results = [next(each) for each in running]
+    return results
+
+
+def iterate_kernel(
+    high_ref, low_ref, start_ref, own_ref, out_ref, rows_ref, images_ref, gram_ref, factor_ref, joint
+):
+    rank, tokens = start_ref.shape
+    scale = 1.0 / (tokens * joint)
+    left, right = slice(0, rank // 2), slice(rank // 2, rank)
+
+    def applied(rows):
+        rows_high, rows_low = halves_of(rows)
+        return (
+            dot_of(rows_high, high_ref[...], 1, 0)
+            + dot_of(rows_high, low_ref[...], 1, 0)
+            + dot_of(rows_low, high_ref[...], 1, 0)
+        )
+
+    def gram_block(rows, images):
+        return thrice(rows, images, 1, 1) * scale
+
+    def reduced(factor):
+        scaled = exact(factor, gram_ref[left, right], 1, 0)
+        return scaled, gram_ref[right, right] - exact(scaled, scaled, 0, 0)
+
+    images = applied(start_ref[...])
+    images_ref[...] = images
+    gram = gram_block(start_ref[...], images)
+    gram_ref[...] = gram
+    factor_ref[...] = factors_of(gram[left, left])[0]
 
     def step(iteration, carry):
-        rows_high, rows_low = halves_of(rows_ref[...])
-        images = (
-            dot_of(high_ref[...], rows_high, 1, 0)
-            + dot_of(high_ref[...], rows_low, 1, 0)
-            + dot_of(low_ref[...], rows_high, 1, 0)
-        )
-        images_high, images_low = halves_of(images)
-        gram_ref[...] = (
-            dot_of(rows_high, images_high, 0, 0)
-            + dot_of(rows_high, images_low, 0, 0)
-            + dot_of(rows_low, images_high, 0, 0)
-        ) * (1.0 / (tokens * joint))
-
-        @pl.when(iteration < ITERS - 1)
-        def _():
-            rows_ref[...] = images
-
-        for panel in range(panels):
-            start, end = panel * LANES, (panel + 1) * LANES
-            inverse = inverse_factor(gram_ref[start:end, start:end])
-            columns = thrice(rows_ref[:, start:end], inverse, 1, 1)
-            rows_ref[:, start:end] = columns
-            if end < rank:
-                scaled = exact(inverse, gram_ref[start:end, end:], 1, 0)
-                gram_ref[end:, end:] -= exact(scaled, scaled, 0, 0)
-                rows_ref[:, end:] -= thrice(columns, scaled, 1, 0)
+        factor = factor_ref[...]
+        scaled, rest = reduced(factor)
+        first = thrice(factor, images_ref[left, :], 1, 0)
+        first_images = applied(first)
+        rest_factor, next_factor = factors_of(rest, gram_block(first, first_images))
+        remaining = images_ref[right, :] - thrice(scaled, first, 0, 0)
+        second = thrice(rest_factor, remaining, 1, 0)
+        second_images = applied(second)
+        rows_ref[left, :] = first
+        rows_ref[right, :] = second
+        gram_ref[left, right] = gram_block(first, second_images)
+        gram_ref[right, right] = gram_block(second, second_images)
+        images_ref[left, :] = first_images
+        images_ref[right, :] = second_images
+        factor_ref[...] = next_factor
         return carry
 
-    lax.fori_loop(0, ITERS, step, 0)
+    lax.fori_loop(0, ITERS - 1, step, 0)
     rows_high, rows_low = halves_of(rows_ref[...])
     own = own_ref[...]
-    out_ref[...] = (dot_of(own, rows_high, 0, 0) + dot_of(own, rows_low, 0, 0)) * (1.0 / tokens)
+    loose = (dot_of(rows_high, own, 1, 0) + dot_of(rows_low, own, 1, 0)) * (1.0 / tokens)
+    factor = factor_ref[...]
+    scaled, rest = reduced(factor)
+    first = thrice(factor, loose[left, :], 1, 0)
+    out_ref[:, left] = thrice(loose[left, :], factor, 0, 1)
+    second = loose[right, :] - thrice(scaled, first, 0, 0)
+    out_ref[:, right] = thrice(second, factors_of(rest)[0], 0, 1)
 
 
 def iterate(high, low, start, own, joint):
-    tokens, rank = start.shape
+    rank, tokens = start.shape
 
     def kernel(*refs):
         iterate_kernel(*refs, joint)
@@ -233,8 +267,10 @@
         in_specs=[pl.BlockSpec(memory_space=pltpu.VMEM)] * 4,
         out_specs=pl.BlockSpec(memory_space=pltpu.VMEM),
         scratch_shapes=[
-            pltpu.VMEM((tokens, rank), jnp.float32),
+            pltpu.VMEM((rank, tokens), jnp.float32),
+            pltpu.VMEM((rank, tokens), jnp.float32),
             pltpu.VMEM((rank, rank), jnp.float32),
+            pltpu.VMEM((rank // 2, rank // 2), jnp.float32),
         ],
         compiler_params=pltpu.CompilerParams(vmem_limit_bytes=40 * 2**20),
     )(high, low, start, own)
@@ -427,11 +463,11 @@
             area = slice(start, start + strip)
             part = out_ref[area, pl.ds(place, width)]
             product = dot_of(part, block, 1, 1)
-            rows = dot_of(part, basis_high, 1, 0) + dot_of(part, basis_low, 1, 0)
+            rows = dot_of(basis_high, part, 0, 1) + dot_of(basis_low, part, 0, 1)
             if turn:
                 product = product + token_sums[area, :]
-                rows = rows + rows_ref[area, :]
-            rows_ref[area, :] = rows
+                rows = rows + rows_ref[:, area]
+            rows_ref[:, area] = rows
             if turn < heads - 1:
                 token_sums[area, :] = product
             else:
@@ -556,7 +592,7 @@
         out_shape=(
             jax.ShapeDtypeStruct((tokens, tokens), jnp.bfloat16),
             jax.ShapeDtypeStruct((tokens, tokens), jnp.bfloat16),
-            jax.ShapeDtypeStruct((tokens, basis.shape[1]), jnp.float32),
+            jax.ShapeDtypeStruct((basis.shape[1], tokens), jnp.float32),
             jax.ShapeDtypeStruct((tokens, width), jnp.bfloat16),
         ),
         in_specs=[anywhere] * 4 + [inside] * 2 + [anywhere],

time: 93.7 us -> 79.5 us (0.85)
  Pallas kernels: 90.5 us -> 76.3 us
    pallas_call x1, Pallas kernels: 42.4 us -> 27.9 us  [iterate(): pl.pallas_call(kernel, out_shape=jax.ShapeDtypeStruct((own.shape[1], rank...]
where the time goes in v4:
time: 79.5 us; the launch traced here: 79.2 us
  Pallas kernels  76.3 us (96%)
  local copies, waits for them, and re-layouts  1.79 us (2%)
  other arithmetic  1.08 us (1%)
    pallas_call x1, Pallas kernels, collect(): pl.pallas_call(functools.partial(collect_kernel, heads), out_shape=(jax.S...  48.4 us
    pallas_call x1, Pallas kernels, iterate(): pl.pallas_call(kernel, out_shape=jax.ShapeDtypeStruct((own.shape[1], rank...  27.9 us
    unnamed x4, local copies, waits for them, and re-layouts  1.79 us

profile of v4, /device:TPU:0, one launch (start us, length us, event | category | flops | bytes accessed | tf_op | source)
XLA Modules:
  0.0 79.2 jit_solution(10655776381183988303)
XLA Ops:
  0.0 0.7 convert_bitcast_fusion
  0.7 0.3 fusion
  1.0 0.1 pad_maximum_fusion
  1.1 0.0 copy-start
  1.1 1.0 %copy-done = f32[512,256]{1,0:T(8,128)S(1)} copy-done((f32[512,256]{1,0:T(8,128)S(1)}, f32[512,256]{1,0:T(8,128)}, u32[]{:S(2)}) %copy-start) | copy-done | bytes 524312
  2.1 0.0 copy-start.1
  2.1 0.8 copy-done.1
  2.9 48.4 %shard_map.64 = (bf16[1024,1024]{1,0:T(8,128)(2,1)S(1)}, bf16[1024,1024]{1,0:T(8,128)(2,1)S(1)}, f32[256,1024]{1,0:T(8,128)S(1)}, bf16[1024,512]{1,0:T(8,128)(2,1)S(1)}) custom-call(bf16[256,8192]{1,0:T(8,128)(2,1)} %bitcast.5, f32[1,8192]{1,0:T(1,128)S(1)} %bitcast.4, bf16[8192,256]{1,0:T(8,128)(2,1)} %key_ref.1, bf16[8192,256]{1,0:T(8,128)(2,1)} %value_ref.1, ...), custom_call_target="tpu_custom_call" | custom-call | tf_op jit(solution)/shard_map/pallas_call | solution.py:590
  51.3 27.9 %shard_map.65 = f32[512,256]{1,0:T(8,128)} custom-call(bf16[1024,1024]{1,0:T(8,128)(2,1)S(1)} %get-tuple-element.9.refs_0_, bf16[1024,1024]{1,0:T(8,128)(2,1)S(1)} %get-tuple-element.10.refs_1_, f32[256,1024]{1,0:T(8,128)S(1)} %get-tuple-element.11.refs_2_, bf16[1024,512]{1,0:T(8,128)(2,1)S(1)} %get-tuple-element.12.refs_3_), custom_call_target="tpu_custom_call" | custom-call | tf_op jit(solution)/shard_map/pallas_call | solution.py:264
  (1 shorter events, 0.0 us)
Async XLA Ops:
  1.1 1.0 %copy-start = (f32[512,256]{1,0:T(8,128)S(1)}, f32[512,256]{1,0:T(8,128)}, u32[]{:S(2)}) copy-start(f32[512,256]{1,0:T(8,128)} %basis_ref.1) | copy-start | bytes 1572868
  2.1 0.8 copy-start.1

commit v5 on v4

--- a/solution.py
+++ b/solution.py
@@ -314,7 +314,7 @@
     local, width = peer_partial.shape
     half = width // 2
     rank = whole_ref.shape[1]
-    piece = width // 8
+    piece = width // 4
     depth = gain_row.shape[1]
     chunks = load_sems.shape[1]
     chunk = depth // chunks
@@ -366,7 +366,7 @@
     for c in range(chunks):
         away_loads[c].start()
         key_loads[c].start()
-    for load in value_loads + mine_loads:
+    for load in mine_loads + value_loads:
         load.start()
 
     barrier = pltpu.get_barrier_semaphore()
@@ -385,14 +385,14 @@
             device_id_type=pl.DeviceIdType.MESH,
         )
 
-    def region(xs, bs, zs, start=0, size=width):
+    def region(kind, xs, bs, zs, start=0, size=half):
         row = pl.multiple_of((xs * 4 + bs) * local, local)
-        column = pl.multiple_of(zs * width + start, half)
+        column = pl.multiple_of(zs * width + (half if kind else 0) + start, LANES)
         return out_ref.at[pl.ds(row, local), pl.ds(column, size)]
 
-    def piece_of(xs, bs, zs, start=0, size=rank):
-        row = pl.multiple_of(zs * width + (xs * 4 + bs) * piece, piece)
-        return whole_ref.at[pl.ds(row, piece), pl.ds(start, size)]
+    def piece_of(bs, zs):
+        row = pl.multiple_of(zs * width + bs * piece, piece)
+        return whole_ref.at[pl.ds(row, piece), :]
 
     started = []
 
@@ -416,49 +416,68 @@
         going.start()
         started.append(going)
 
-    def spread(kind, area, middle, turn):
-        s = sources[turn]
-        own = area(x, b, s)
+    cuts = (half // 2, 0, half)
+
+    def spread(kind, turn):
+        own = region(kind, x, b, sources[turn])
         if turn:
-            arrive(own, z_sems.at[kind, s], z_peer(turn))
+            arrive(own, z_sems.at[kind, sources[turn]], z_peer(turn))
         send(own, x_sems.at[kind, turn], x_peer)
         send(own, y_sems.at[kind, turn], y_peer)
         send(own, core_sems.at[kind, turn, 0], core_peer)
 
-    def relay(kind, area, middle, turn):
-        s = sources[turn]
-        arrive(area(other_x, b, s), x_sems.at[kind, turn], x_peer)
-        beyond = area(other_x, b, s, middle, middle) if middle else area(other_x, b, s)
-        send(beyond, y_half_sems.at[kind, turn], y_peer)
-        send(area(other_x, b, s), core_sems.at[kind, turn, 1], core_peer)
-        arrive(area(x, other_y, s), y_sems.at[kind, turn], y_peer)
-        if middle:
-            send(area(x, other_y, s, 0, middle), x_half_sems.at[kind, turn], x_peer)
-        send(area(x, other_y, s), core_sems.at[kind, turn, 2], core_peer)
-
-    def finish(kind, area, middle, turn):
-        s = sources[turn]
-        if middle:
-            arrive(area(other_x, other_y, s, 0, middle), x_half_sems.at[kind, turn], x_peer)
-        beyond = area(other_x, other_y, s, middle, middle) if middle else area(other_x, other_y, s)
-        arrive(beyond, y_half_sems.at[kind, turn], y_peer)
-        send(area(other_x, other_y, s), core_sems.at[kind, turn, 3], core_peer)
+    def relay(kind, turn):
+        s, cut = sources[turn], cuts[kind]
+        arrive(region(kind, other_x, b, s), x_sems.at[kind, turn], x_peer)
+        if cut < half:
+            beyond = region(kind, other_x, b, s, cut, half - cut)
+            send(beyond, y_half_sems.at[kind, turn], y_peer)
+        send(region(kind, other_x, b, s), core_sems.at[kind, turn, 1], core_peer)
+        arrive(region(kind, x, other_y, s), y_sems.at[kind, turn], y_peer)
+        send(region(kind, x, other_y, s, 0, cut), x_half_sems.at[kind, turn], x_peer)
+        send(region(kind, x, other_y, s), core_sems.at[kind, turn, 2], core_peer)
+
+    def finish(kind, turn):
+        s, cut = sources[turn], cuts[kind]
+        arrive(region(kind, other_x, other_y, s, 0, cut), x_half_sems.at[kind, turn], x_peer)
+        if cut < half:
+            beyond = region(kind, other_x, other_y, s, cut, half - cut)
+            arrive(beyond, y_half_sems.at[kind, turn], y_peer)
+        send(region(kind, other_x, other_y, s), core_sems.at[kind, turn, 3], core_peer)
 
     far = (partner + 2) % 4
 
-    def gathered(kind, area, middle, turn):
+    def gathered(kind, turn):
         places = [(x, partner), (other_x, partner), (x, far), (other_x, far)]
         for place, (xs, bs) in enumerate(places):
-            arrive(area(xs, bs, sources[turn]), core_sems.at[kind, turn, place], core_peer)
-
-    joint = [(0, region, half, turn) for turn in range(heads)]
-    pieces = [(1, piece_of, 0, turn) for turn in range(1, heads)]
+            area = region(kind, xs, bs, sources[turn])
+            arrive(area, core_sems.at[kind, turn, place], core_peer)
+
+    def spread_basis(turn):
+        own = piece_of(b, sources[turn])
+        arrive(own, z_sems.at[1, sources[turn]], z_peer(turn))
+        send(own, y_sems.at[1, turn], y_peer)
+        send(own, core_sems.at[1, turn, 0], core_peer)
+
+    def relay_basis(turn):
+        other = piece_of(other_y, sources[turn])
+        arrive(other, y_sems.at[1, turn], y_peer)
+        send(other, core_sems.at[1, turn, 1], core_peer)
+
+    def gathered_basis(turn):
+        arrive(piece_of(partner, sources[turn]), core_sems.at[1, turn, 0], core_peer)
+        arrive(piece_of(far, sources[turn]), core_sems.at[1, turn, 1], core_peer)
+
     tokens, strip = out_ref.shape[0], 256
 
     def accumulate(turn):
         place = pl.multiple_of(sources[turn] * width, width)
         block = out_ref[:, pl.ds(place, width)]
-        basis_high, basis_low = halves_of(whole_ref[pl.ds(place, width), :])
+        basis_block = whole_ref[pl.ds(place, width), :]
+        spots = [slice(at, at + HEAD_DIM) for at in range(0, width, HEAD_DIM)]
+        spots = spots[0::2] + spots[1::2]
+        basis_block = jnp.concatenate([basis_block[spot, :] for spot in spots], axis=0)
+        basis_high, basis_low = halves_of(basis_block)
         for start in range(0, tokens, strip):
             area = slice(start, start + strip)
             part = out_ref[area, pl.ds(place, width)]
@@ -475,11 +494,12 @@
                 high_ref[area, :] = high
                 low_ref[area, :] = low
             if turn == 0:
-                own_ref[area, :] = part
+                for index, spot in enumerate(spots):
+                    own_ref[area, spot] = part[:, index * HEAD_DIM : (index + 1) * HEAD_DIM]
 
     basis_load.wait()
     for turn in range(1, heads):
-        send_z(piece_of(x, b, z), 1, turn)
+        send_z(piece_of(b, z), 1, turn)
 
     def prepare(area, c, total):
         widened = hidden_rows[area, span(c)].astype(jnp.float32)
@@ -513,27 +533,13 @@
         swap(squares, peer_squares, 0),
         swap(partial.at[:, pl.ds(0, half)], peer_partial.at[:, pl.ds(0, half)], 1),
     ]
-    for item in pieces:
-        spread(*item)
+    mine_total = jnp.zeros((local, LANES), jnp.float32)
     sums = jnp.zeros((local, half), jnp.float32)
-    for c in range(chunks):
-        value_loads[c].wait()
-        sums = sums + dot_of(hidden_rows[away, span(c)], value_rows[span(c), :], 1, 0)
-    partial[:, half:] = sums
-    swaps.append(swap(partial.at[:, pl.ds(half, half)], peer_partial.at[:, pl.ds(half, half)], 2))
-    for item in pieces:
-        relay(*item)
-    mine_total = jnp.zeros((local, LANES), jnp.float32)
-    key_sums = jnp.zeros((local, half), jnp.float32)
-    value_sums = jnp.zeros((local, half), jnp.float32)
     for c in range(chunks):
         mine_loads[c].wait()
         scaled, mine_total = prepare(mine, c, mine_total)
-        key_sums = key_sums + dot_of(scaled, key_rows[span(c), :], 1, 0)
-        value_sums = value_sums + dot_of(scaled, value_rows[span(c), :], 1, 0)
+        sums = sums + dot_of(scaled, key_rows[span(c), :], 1, 0)
     own_squares = across(mine_total)
-    for item in pieces:
-        finish(*item)
 
     swaps[0].wait()
     eighths = jnp.full((SUBLANES, LANES), 1.0 / SUBLANES, jnp.float32)
@@ -542,33 +548,64 @@
     swaps[1].wait()
     for g in range(half // HEAD_DIM):
         spot = slice(g * HEAD_DIM, (g + 1) * HEAD_DIM)
-        key = (key_sums[:, spot] + peer_partial[:, spot]) * inverse_scale
+        key = (sums[:, spot] + peer_partial[:, spot]) * inverse_scale
         turned = key * cosine_ref[...] + pltpu.roll(key, HEAD_DIM // 2, 1) * sine_ref[...]
-        column = pl.multiple_of(z * width + 2 * g * HEAD_DIM, HEAD_DIM)
+        column = pl.multiple_of(z * width + g * HEAD_DIM, HEAD_DIM)
         out_ref[pl.ds(row, local), pl.ds(column, HEAD_DIM)] = turned.astype(jnp.bfloat16)
-    swaps[2].wait()
-    for g in range(half // HEAD_DIM):
-        spot = slice(g * HEAD_DIM, (g + 1) * HEAD_DIM)
-        there = slice(half + g * HEAD_DIM, half + (g + 1) * HEAD_DIM)
-        value = (value_sums[:, spot] + peer_partial[:, there]) * inverse_scale
-        column = pl.multiple_of(z * width + (2 * g + 1) * HEAD_DIM, HEAD_DIM)
-        out_ref[pl.ds(row, local), pl.ds(column, HEAD_DIM)] = value.astype(jnp.bfloat16)
-
     for turn in range(1, heads):
-        send_z(region(x, b, z), 0, turn)
-    for turn in range(len(joint) + 3):
-        if turn < len(joint):
-            spread(*joint[turn])
-        if 1 <= turn < len(joint) + 1:
-            relay(*joint[turn - 1])
-        if 2 <= turn < len(joint) + 2:
-            finish(*joint[turn - 2])
-        if turn == 2:
-            for item in pieces:
-                gathered(*item)
-        if turn >= 3:
-            gathered(*joint[turn - 3])
-            accumulate(turn - 3)
+        send_z(region(0, x, b, z), 0, turn)
+    spread(0, 0)
+
+    sums = jnp.zeros((local, half), jnp.float32)
+    for c in range(chunks):
+        value_loads[c].wait()
+        sums = sums + dot_of(hidden_rows[away, span(c)], value_rows[span(c), :], 1, 0)
+    partial[:, half:] = sums
+    swaps.append(swap(partial.at[:, pl.ds(half, half)], peer_partial.at[:, pl.ds(half, half)], 2))
+    sums = jnp.zeros((local, half), jnp.float32)
+    for c in range(chunks):
+        sums = sums + dot_of(hidden_rows[mine, span(c)], value_rows[span(c), :], 1, 0)
+
+    def values():
+        swaps[2].wait()
+        for g in range(half // HEAD_DIM):
+            spot = slice(g * HEAD_DIM, (g + 1) * HEAD_DIM)
+            there = slice(half + g * HEAD_DIM, half + (g + 1) * HEAD_DIM)
+            value = (sums[:, spot] + peer_partial[:, there]) * inverse_scale
+            column = pl.multiple_of(z * width + half + g * HEAD_DIM, HEAD_DIM)
+            out_ref[pl.ds(row, local), pl.ds(column, HEAD_DIM)] = value.astype(jnp.bfloat16)
+        for turn in range(1, heads):
+            send_z(region(2, x, b, z), 2, turn)
+
+    keys_first = min(2, heads)
+    items = [(0, turn) for turn in range(keys_first)] + [(2, 0)]
+    items += [(0, turn) for turn in range(keys_first, heads)]
+    items += [(2, turn) for turn in range(1, heads)]
+
+    def complete(kind, turn):
+        gathered(kind, turn)
+        if kind:
+            accumulate(turn)
+
+    for step in range(1, len(items) + 3):
+        if step < len(items):
+            if items[step] == (2, 0):
+                values()
+            spread(*items[step])
+            if items[step] == (2, 0):
+                for turn in range(1, heads):
+                    spread_basis(turn)
+        if step < len(items) + 1:
+            relay(*items[step - 1])
+        if step == len(items) - 1:
+            for turn in range(1, heads):
+                relay_basis(turn)
+            for turn in range(1, heads):
+                gathered_basis(turn)
+        if step >= 3:
+            complete(*items[step - 3])
+        if 2 <= step < len(items) + 2:
+            finish(*items[step - 2])
     for going in started:
         going.wait_send()
 
@@ -612,24 +649,24 @@
             dma((2, chunks)),
             dma((3, chunks)),
             dma((3, 2)),
-            dma((2, heads, 2)),
-            dma((2, heads, 2)),
-            dma((2, heads, 2)),
-            dma((2, heads, 2)),
-            dma((2, heads, 2)),
-            dma((2, heads, 4, 2)),
+            dma((3, heads, 2)),
+            dma((3, heads, 2)),
+            dma((3, heads, 2)),
+            dma((3, heads, 2)),
+            dma((3, heads, 2)),
+            dma((3, heads, 4, 2)),
         ],
         compiler_params=pltpu.CompilerParams(
             collective_id=0, has_side_effects=True, vmem_limit_bytes=45 * 2**20
         ),
     )(
         hidden_rows,
-        gain[None, :],
+        pltpu.with_memory_space_constraint(gain[None, :], pltpu.HBM),
         key_weight,
         value_weight,
         jnp.concatenate([cosine, cosine], axis=1),
         jnp.concatenate([-sine, sine], axis=1),
-        basis,
+        pltpu.with_memory_space_constraint(basis, pltpu.HBM),
     )
 
 

time: 79.5 us -> 86.9 us (1.093)
  the two profiles are of different devices: /device:TPU:0 before, /device:TPU:17 now
where the time goes in v5:
time: 86.9 us; the launch traced here: 86.7 us
  Pallas kernels  85.6 us (99%)
  other arithmetic  1.08 us (1%)
    pallas_call x1, Pallas kernels, collect(): pl.pallas_call(functools.partial(collect_kernel, heads), out_shape=(jax.S...  57.9 us
    pallas_call x1, Pallas kernels, iterate(): pl.pallas_call(kernel, out_shape=jax.ShapeDtypeStruct((own.shape[1], rank...  27.7 us

profile of v5, /device:TPU:17, one launch (start us, length us, event | category | flops | bytes accessed | tf_op | source)
XLA Modules:
  0.0 86.7 jit_solution(15179571635310524126)
XLA Ops:
  0.0 0.7 convert_bitcast_fusion
  0.7 0.3 fusion
  1.0 0.1 pad_maximum_fusion
  1.1 57.9 %shard_map.64 = (bf16[1024,1024]{1,0:T(8,128)(2,1)S(1)}, bf16[1024,1024]{1,0:T(8,128)(2,1)S(1)}, f32[256,1024]{1,0:T(8,128)S(1)}, bf16[1024,512]{1,0:T(8,128)(2,1)S(1)}) custom-call(bf16[256,8192]{1,0:T(8,128)(2,1)} %bitcast.4, f32[1,8192]{1,0:T(1,128)} %bitcast.5, bf16[8192,256]{1,0:T(8,128)(2,1)} %key_ref.1, bf16[8192,256]{1,0:T(8,128)(2,1)} %value_ref.1, ...), custom_call_target="tpu_custom_call" | custom-call | tf_op jit(solution)/shard_map/pallas_call | solution.py:627
  59.0 27.7 %shard_map.65 = f32[512,256]{1,0:T(8,128)} custom-call(bf16[1024,1024]{1,0:T(8,128)(2,1)S(1)} %get-tuple-element.9.refs_0_, bf16[1024,1024]{1,0:T(8,128)(2,1)S(1)} %get-tuple-element.10.refs_1_, f32[256,1024]{1,0:T(8,128)S(1)} %get-tuple-element.11.refs_2_, bf16[1024,512]{1,0:T(8,128)(2,1)S(1)} %get-tuple-element.12.refs_3_), custom_call_target="tpu_custom_call" | custom-call | tf_op jit(solution)/shard_map/pallas_call | solution.py:264
  (1 shorter events, 0.0 us)

commit v6 on v4

--- a/solution.py
+++ b/solution.py
@@ -363,11 +363,20 @@
     ]
     basis_load.start()
     gain_load.start()
-    for c in range(chunks):
-        away_loads[c].start()
-        key_loads[c].start()
-    for load in value_loads + mine_loads:
-        load.start()
+    loads = [load for pair in zip(away_loads, key_loads) for load in pair]
+    loads += value_loads + mine_loads
+    waiting = list(loads)
+
+    def issue():
+        if waiting:
+            waiting.pop(0).start()
+
+    def ready(load):
+        load.wait()
+        issue()
+
+    for _ in range(4):
+        issue()
 
     barrier = pltpu.get_barrier_semaphore()
     peers = [x_peer, y_peer, core_peer] + [z_peer(d) for d in range(1, heads)]
@@ -462,18 +471,18 @@
         for start in range(0, tokens, strip):
             area = slice(start, start + strip)
             part = out_ref[area, pl.ds(place, width)]
-            product = dot_of(part, block, 1, 1)
+            product = dot_of(block, part, 1, 1)
             rows = dot_of(basis_high, part, 0, 1) + dot_of(basis_low, part, 0, 1)
             if turn:
-                product = product + token_sums[area, :]
+                product = product + token_sums[:, area]
                 rows = rows + rows_ref[:, area]
             rows_ref[:, area] = rows
             if turn < heads - 1:
-                token_sums[area, :] = product
+                token_sums[:, area] = product
             else:
                 high, low = halves_of(product * (1.0 / tokens))
-                high_ref[area, :] = high
-                low_ref[area, :] = low
+                high_ref[:, area] = high
+                low_ref[:, area] = low
             if turn == 0:
                 own_ref[area, :] = part
 
@@ -503,9 +512,9 @@
     away_total = jnp.zeros((local, LANES), jnp.float32)
     sums = jnp.zeros((local, half), jnp.float32)
     for c in range(chunks):
-        away_loads[c].wait()
+        ready(away_loads[c])
         scaled, away_total = prepare(away, c, away_total)
-        key_loads[c].wait()
+        ready(key_loads[c])
         sums = sums + dot_of(scaled, key_rows[span(c), :], 1, 0)
     partial[:, :half] = sums
     squares[...] = across(away_total)
@@ -513,27 +522,23 @@
         swap(squares, peer_squares, 0),
         swap(partial.at[:, pl.ds(0, half)], peer_partial.at[:, pl.ds(0, half)], 1),
     ]
-    for item in pieces:
-        spread(*item)
     sums = jnp.zeros((local, half), jnp.float32)
     for c in range(chunks):
-        value_loads[c].wait()
+        ready(value_loads[c])
         sums = sums + dot_of(hidden_rows[away, span(c)], value_rows[span(c), :], 1, 0)
     partial[:, half:] = sums
     swaps.append(swap(partial.at[:, pl.ds(half, half)], peer_partial.at[:, pl.ds(half, half)], 2))
-    for item in pieces:
-        relay(*item)
     mine_total = jnp.zeros((local, LANES), jnp.float32)
     key_sums = jnp.zeros((local, half), jnp.float32)
     value_sums = jnp.zeros((local, half), jnp.float32)
     for c in range(chunks):
-        mine_loads[c].wait()
+        ready(mine_loads[c])
         scaled, mine_total = prepare(mine, c, mine_total)
         key_sums = key_sums + dot_of(scaled, key_rows[span(c), :], 1, 0)
         value_sums = value_sums + dot_of(scaled, value_rows[span(c), :], 1, 0)
     own_squares = across(mine_total)
     for item in pieces:
-        finish(*item)
+        spread(*item)
 
     swaps[0].wait()
     eighths = jnp.full((SUBLANES, LANES), 1.0 / SUBLANES, jnp.float32)
@@ -556,19 +561,31 @@
 
     for turn in range(1, heads):
         send_z(region(x, b, z), 0, turn)
-    for turn in range(len(joint) + 3):
+    for turn in range(len(joint) + 2):
         if turn < len(joint):
             spread(*joint[turn])
         if 1 <= turn < len(joint) + 1:
             relay(*joint[turn - 1])
-        if 2 <= turn < len(joint) + 2:
+        if turn == len(joint) + 1:
+            for item in pieces:
+                gathered(*item)
+            for early in range(1, len(joint) - 2):
+                gathered(*joint[early])
+                accumulate(early)
+        if turn >= 2:
             finish(*joint[turn - 2])
+        if turn == 1:
+            for item in pieces:
+                relay(*item)
         if turn == 2:
             for item in pieces:
-                gathered(*item)
-        if turn >= 3:
-            gathered(*joint[turn - 3])
-            accumulate(turn - 3)
+                finish(*item)
+        if turn == 3:
+            gathered(*joint[0])
+            accumulate(0)
+    for turn in range(max(1, len(joint) - 2), len(joint)):
+        gathered(*joint[turn])
+        accumulate(turn)
     for going in started:
         going.wait_send()
 
@@ -624,12 +641,12 @@
         ),
     )(
         hidden_rows,
-        gain[None, :],
+        pltpu.with_memory_space_constraint(gain[None, :], pltpu.HBM),
         key_weight,
         value_weight,
         jnp.concatenate([cosine, cosine], axis=1),
         jnp.concatenate([-sine, sine], axis=1),
-        basis,
+        pltpu.with_memory_space_constraint(basis, pltpu.HBM),
     )
 
 

time: 79.5 us -> 75.9 us (0.955)
  local copies, waits for them, and re-layouts: 1.79 us -> 0 us
  Pallas kernels: 76.3 us -> 74.6 us
    unnamed x4 -> x0, local copies, waits for them, and re-layouts: 1.79 us -> none
    pallas_call x1, Pallas kernels: 48.4 us -> 46.9 us  [collect(): pl.pallas_call(functools.partial(collect_kernel, heads), out_shape=(jax.S...]
where the time goes in v6:
time: 75.9 us; the launch traced here: 75.7 us
  Pallas kernels  74.6 us (98%)
  other arithmetic  1.08 us (1%)
    pallas_call x1, Pallas kernels, collect(): pl.pallas_call(functools.partial(collect_kernel, heads), out_shape=(jax.S...  46.9 us
    pallas_call x1, Pallas kernels, iterate(): pl.pallas_call(kernel, out_shape=jax.ShapeDtypeStruct((own.shape[1], rank...  27.7 us

profile of v6, /device:TPU:0, one launch (start us, length us, event | category | flops | bytes accessed | tf_op | source)
XLA Modules:
  0.0 75.7 jit_solution(15789092116185887734)
XLA Ops:
  0.0 0.7 convert_bitcast_fusion
  0.7 0.3 fusion
  1.0 0.1 pad_maximum_fusion
  1.1 46.9 %shard_map.64 = (bf16[1024,1024]{1,0:T(8,128)(2,1)S(1)}, bf16[1024,1024]{1,0:T(8,128)(2,1)S(1)}, f32[256,1024]{1,0:T(8,128)S(1)}, bf16[1024,512]{1,0:T(8,128)(2,1)S(1)}) custom-call(bf16[256,8192]{1,0:T(8,128)(2,1)} %bitcast.4, f32[1,8192]{1,0:T(1,128)} %bitcast.5, bf16[8192,256]{1,0:T(8,128)(2,1)} %key_ref.1, bf16[8192,256]{1,0:T(8,128)(2,1)} %value_ref.1, ...), custom_call_target="tpu_custom_call" | custom-call | tf_op jit(solution)/shard_map/pallas_call | solution.py:607
  48.0 27.7 %shard_map.65 = f32[512,256]{1,0:T(8,128)} custom-call(bf16[1024,1024]{1,0:T(8,128)(2,1)S(1)} %get-tuple-element.9.refs_0_, bf16[1024,1024]{1,0:T(8,128)(2,1)S(1)} %get-tuple-element.10.refs_1_, f32[256,1024]{1,0:T(8,128)S(1)} %get-tuple-element.11.refs_2_, bf16[1024,512]{1,0:T(8,128)(2,1)S(1)} %get-tuple-element.12.refs_3_), custom_call_target="tpu_custom_call" | custom-call | tf_op jit(solution)/shard_map/pallas_call | solution.py:264
  (1 shorter events, 0.0 us)

commit v7 on v6

--- a/solution.py
+++ b/solution.py
@@ -375,7 +375,7 @@
         load.wait()
         issue()
 
-    for _ in range(4):
+    for _ in range(6):
         issue()
 
     barrier = pltpu.get_barrier_semaphore()
@@ -537,8 +537,6 @@
         key_sums = key_sums + dot_of(scaled, key_rows[span(c), :], 1, 0)
         value_sums = value_sums + dot_of(scaled, value_rows[span(c), :], 1, 0)
     own_squares = across(mine_total)
-    for item in pieces:
-        spread(*item)
 
     swaps[0].wait()
     eighths = jnp.full((SUBLANES, LANES), 1.0 / SUBLANES, jnp.float32)
@@ -564,28 +562,29 @@
     for turn in range(len(joint) + 2):
         if turn < len(joint):
             spread(*joint[turn])
+        if turn == 0:
+            for item in pieces:
+                spread(*item)
         if 1 <= turn < len(joint) + 1:
             relay(*joint[turn - 1])
         if turn == len(joint) + 1:
             for item in pieces:
                 gathered(*item)
-            for early in range(1, len(joint) - 2):
+            for early in range(1, len(joint) - 1):
                 gathered(*joint[early])
                 accumulate(early)
         if turn >= 2:
             finish(*joint[turn - 2])
-        if turn == 1:
+        if turn == 2:
             for item in pieces:
                 relay(*item)
-        if turn == 2:
+        if turn == 3:
             for item in pieces:
                 finish(*item)
-        if turn == 3:
             gathered(*joint[0])
             accumulate(0)
-    for turn in range(max(1, len(joint) - 2), len(joint)):
-        gathered(*joint[turn])
-        accumulate(turn)
+    gathered(*joint[-1])
+    accumulate(len(joint) - 1)
     for going in started:
         going.wait_send()
 

time: 75.9 us -> 78.5 us (1.034)
  Pallas kernels: 74.6 us -> 76.7 us
    pallas_call x1, Pallas kernels: 46.9 us -> 48.9 us  [collect(): pl.pallas_call(functools.partial(collect_kernel, heads), out_shape=(jax.S...]
where the time goes in v7:
time: 78.5 us; the launch traced here: 77.8 us
  Pallas kernels  76.7 us (98%)
  other arithmetic  1.08 us (1%)
    pallas_call x1, Pallas kernels, collect(): pl.pallas_call(functools.partial(collect_kernel, heads), out_shape=(jax.S...  48.9 us
    pallas_call x1, Pallas kernels, iterate(): pl.pallas_call(kernel, out_shape=jax.ShapeDtypeStruct((own.shape[1], rank...  27.7 us

profile of v7, /device:TPU:0, one launch (start us, length us, event | category | flops | bytes accessed | tf_op | source)
XLA Modules:
  0.0 77.8 jit_solution(13860006248805565654)
XLA Ops:
  0.0 0.7 convert_bitcast_fusion
  0.7 0.3 fusion
  1.0 0.1 pad_maximum_fusion
  1.1 48.9 %shard_map.64 = (bf16[1024,1024]{1,0:T(8,128)(2,1)S(1)}, bf16[1024,1024]{1,0:T(8,128)(2,1)S(1)}, f32[256,1024]{1,0:T(8,128)S(1)}, bf16[1024,512]{1,0:T(8,128)(2,1)S(1)}) custom-call(bf16[256,8192]{1,0:T(8,128)(2,1)} %bitcast.4, f32[1,8192]{1,0:T(1,128)} %bitcast.5, bf16[8192,256]{1,0:T(8,128)(2,1)} %key_ref.1, bf16[8192,256]{1,0:T(8,128)(2,1)} %value_ref.1, ...), custom_call_target="tpu_custom_call" | custom-call | tf_op jit(solution)/shard_map/pallas_call | solution.py:606
  50.1 27.7 %shard_map.65 = f32[512,256]{1,0:T(8,128)} custom-call(bf16[1024,1024]{1,0:T(8,128)(2,1)S(1)} %get-tuple-element.9.refs_0_, bf16[1024,1024]{1,0:T(8,128)(2,1)S(1)} %get-tuple-element.10.refs_1_, f32[256,1024]{1,0:T(8,128)S(1)} %get-tuple-element.11.refs_2_, bf16[1024,512]{1,0:T(8,128)(2,1)S(1)} %get-tuple-element.12.refs_3_), custom_call_target="tpu_custom_call" | custom-call | tf_op jit(solution)/shard_map/pallas_call | solution.py:264
  (1 shorter events, 0.0 us)

commit v8 on v6

--- a/solution.py
+++ b/solution.py
@@ -314,7 +314,7 @@
     local, width = peer_partial.shape
     half = width // 2
     rank = whole_ref.shape[1]
-    piece = width // 8
+    piece = width // 4
     depth = gain_row.shape[1]
     chunks = load_sems.shape[1]
     chunk = depth // chunks
@@ -375,7 +375,7 @@
         load.wait()
         issue()
 
-    for _ in range(4):
+    for _ in range(6):
         issue()
 
     barrier = pltpu.get_barrier_semaphore()
@@ -399,9 +399,9 @@
         column = pl.multiple_of(zs * width + start, half)
         return out_ref.at[pl.ds(row, local), pl.ds(column, size)]
 
-    def piece_of(xs, bs, zs, start=0, size=rank):
-        row = pl.multiple_of(zs * width + (xs * 4 + bs) * piece, piece)
-        return whole_ref.at[pl.ds(row, piece), pl.ds(start, size)]
+    def piece_of(bs, zs):
+        row = pl.multiple_of(zs * width + bs * piece, piece)
+        return whole_ref.at[pl.ds(row, piece), :]
 
     started = []
 
@@ -460,8 +460,23 @@
         for place, (xs, bs) in enumerate(places):
             arrive(area(xs, bs, sources[turn]), core_sems.at[kind, turn, place], core_peer)
 
+    def spread_basis(turn):
+        own = piece_of(b, sources[turn])
+        arrive(own, z_sems.at[1, sources[turn]], z_peer(turn))
+        send(own, y_sems.at[1, turn], y_peer)
+        send(own, core_sems.at[1, turn, 0], core_peer)
+
+    def relay_basis(turn):
+        other = piece_of(other_y, sources[turn])
+        arrive(other, y_sems.at[1, turn], y_peer)
+        send(other, core_sems.at[1, turn, 1], core_peer)
+
+    def gathered_basis(turn):
+        arrive(piece_of(partner, sources[turn]), core_sems.at[1, turn, 0], core_peer)
+        arrive(piece_of(far, sources[turn]), core_sems.at[1, turn, 1], core_peer)
+
     joint = [(0, region, half, turn) for turn in range(heads)]
-    pieces = [(1, piece_of, 0, turn) for turn in range(1, heads)]
+    others = range(1, heads)
     tokens, strip = out_ref.shape[0], 256
 
     def accumulate(turn):
@@ -488,7 +503,7 @@
 
     basis_load.wait()
     for turn in range(1, heads):
-        send_z(piece_of(x, b, z), 1, turn)
+        send_z(piece_of(b, z), 1, turn)
 
     def prepare(area, c, total):
         widened = hidden_rows[area, span(c)].astype(jnp.float32)
@@ -537,8 +552,8 @@
         key_sums = key_sums + dot_of(scaled, key_rows[span(c), :], 1, 0)
         value_sums = value_sums + dot_of(scaled, value_rows[span(c), :], 1, 0)
     own_squares = across(mine_total)
-    for item in pieces:
-        spread(*item)
+    for turn in others:
+        spread_basis(turn)
 
     swaps[0].wait()
     eighths = jnp.full((SUBLANES, LANES), 1.0 / SUBLANES, jnp.float32)
@@ -567,19 +582,16 @@
         if 1 <= turn < len(joint) + 1:
             relay(*joint[turn - 1])
         if turn == len(joint) + 1:
-            for item in pieces:
-                gathered(*item)
+            for other in others:
+                gathered_basis(other)
             for early in range(1, len(joint) - 2):
                 gathered(*joint[early])
                 accumulate(early)
         if turn >= 2:
             finish(*joint[turn - 2])
         if turn == 1:
-            for item in pieces:
-                relay(*item)
-        if turn == 2:
-            for item in pieces:
-                finish(*item)
+            for other in others:
+                relay_basis(other)
         if turn == 3:
             gathered(*joint[0])
             accumulate(0)

time: 75.9 us -> 77.9 us (1.026)
  Pallas kernels: 74.6 us -> 76.6 us
    pallas_call x1, Pallas kernels: 46.9 us -> 48.9 us  [collect(): pl.pallas_call(functools.partial(collect_kernel, heads), out_shape=(jax.S...]
where the time goes in v8:
time: 77.9 us; the launch traced here: 77.7 us
  Pallas kernels  76.6 us (98%)
  other arithmetic  1.08 us (1%)
    pallas_call x1, Pallas kernels, collect(): pl.pallas_call(functools.partial(collect_kernel, heads), out_shape=(jax.S...  48.9 us
    pallas_call x1, Pallas kernels, iterate(): pl.pallas_call(kernel, out_shape=jax.ShapeDtypeStruct((own.shape[1], rank...  27.7 us

profile of v8, /device:TPU:0, one launch (start us, length us, event | category | flops | bytes accessed | tf_op | source)
XLA Modules:
  0.0 77.7 jit_solution(4028408572665034311)
XLA Ops:
  0.0 0.7 convert_bitcast_fusion
  0.7 0.3 fusion
  1.0 0.1 pad_maximum_fusion
  1.1 48.9 %shard_map.64 = (bf16[1024,1024]{1,0:T(8,128)(2,1)S(1)}, bf16[1024,1024]{1,0:T(8,128)(2,1)S(1)}, f32[256,1024]{1,0:T(8,128)S(1)}, bf16[1024,512]{1,0:T(8,128)(2,1)S(1)}) custom-call(bf16[256,8192]{1,0:T(8,128)(2,1)} %bitcast.4, f32[1,8192]{1,0:T(1,128)} %bitcast.5, bf16[8192,256]{1,0:T(8,128)(2,1)} %key_ref.1, bf16[8192,256]{1,0:T(8,128)(2,1)} %value_ref.1, ...), custom_call_target="tpu_custom_call" | custom-call | tf_op jit(solution)/shard_map/pallas_call | solution.py:619
  50.0 27.7 %shard_map.65 = f32[512,256]{1,0:T(8,128)} custom-call(bf16[1024,1024]{1,0:T(8,128)(2,1)S(1)} %get-tuple-element.9.refs_0_, bf16[1024,1024]{1,0:T(8,128)(2,1)S(1)} %get-tuple-element.10.refs_1_, f32[256,1024]{1,0:T(8,128)S(1)} %get-tuple-element.11.refs_2_, bf16[1024,512]{1,0:T(8,128)(2,1)S(1)} %get-tuple-element.12.refs_3_), custom_call_target="tpu_custom_call" | custom-call | tf_op jit(solution)/shard_map/pallas_call | solution.py:264
  (1 shorter events, 0.0 us)

commit v9 on v8

--- a/solution.py
+++ b/solution.py
@@ -375,7 +375,7 @@
         load.wait()
         issue()
 
-    for _ in range(6):
+    for _ in range(4):
         issue()
 
     barrier = pltpu.get_barrier_semaphore()
@@ -552,8 +552,6 @@
         key_sums = key_sums + dot_of(scaled, key_rows[span(c), :], 1, 0)
         value_sums = value_sums + dot_of(scaled, value_rows[span(c), :], 1, 0)
     own_squares = across(mine_total)
-    for turn in others:
-        spread_basis(turn)
 
     swaps[0].wait()
     eighths = jnp.full((SUBLANES, LANES), 1.0 / SUBLANES, jnp.float32)
@@ -579,6 +577,9 @@
     for turn in range(len(joint) + 2):
         if turn < len(joint):
             spread(*joint[turn])
+        if turn == 0:
+            for other in others:
+                spread_basis(other)
         if 1 <= turn < len(joint) + 1:
             relay(*joint[turn - 1])
         if turn == len(joint) + 1:
@@ -589,7 +590,7 @@
                 accumulate(early)
         if turn >= 2:
             finish(*joint[turn - 2])
-        if turn == 1:
+        if turn == 2:
             for other in others:
                 relay_basis(other)
         if turn == 3:

time: 77.9 us -> 77.6 us (level)
  no operation moved by 1% of the time
where the time goes in v9:
time: 77.6 us; the launch traced here: 77.5 us
  Pallas kernels  76.4 us (98%)
  other arithmetic  1.08 us (1%)
    pallas_call x1, Pallas kernels, collect(): pl.pallas_call(functools.partial(collect_kernel, heads), out_shape=(jax.S...  48.6 us
    pallas_call x1, Pallas kernels, iterate(): pl.pallas_call(kernel, out_shape=jax.ShapeDtypeStruct((own.shape[1], rank...  27.7 us

profile of v9, /device:TPU:0, one launch (start us, length us, event | category | flops | bytes accessed | tf_op | source)
XLA Modules:
  0.0 77.5 jit_solution(5302516399627805273)
XLA Ops:
  0.0 0.7 convert_bitcast_fusion
  0.7 0.3 fusion
  1.0 0.1 pad_maximum_fusion
  1.1 48.6 %shard_map.64 = (bf16[1024,1024]{1,0:T(8,128)(2,1)S(1)}, bf16[1024,1024]{1,0:T(8,128)(2,1)S(1)}, f32[256,1024]{1,0:T(8,128)S(1)}, bf16[1024,512]{1,0:T(8,128)(2,1)S(1)}) custom-call(bf16[256,8192]{1,0:T(8,128)(2,1)} %bitcast.4, f32[1,8192]{1,0:T(1,128)} %bitcast.5, bf16[8192,256]{1,0:T(8,128)(2,1)} %key_ref.1, bf16[8192,256]{1,0:T(8,128)(2,1)} %value_ref.1, ...), custom_call_target="tpu_custom_call" | custom-call | tf_op jit(solution)/shard_map/pallas_call | solution.py:620
  49.8 27.7 %shard_map.65 = f32[512,256]{1,0:T(8,128)} custom-call(bf16[1024,1024]{1,0:T(8,128)(2,1)S(1)} %get-tuple-element.9.refs_0_, bf16[1024,1024]{1,0:T(8,128)(2,1)S(1)} %get-tuple-element.10.refs_1_, f32[256,1024]{1,0:T(8,128)S(1)} %get-tuple-element.11.refs_2_, bf16[1024,512]{1,0:T(8,128)(2,1)S(1)} %get-tuple-element.12.refs_3_), custom_call_target="tpu_custom_call" | custom-call | tf_op jit(solution)/shard_map/pallas_call | solution.py:264
  (1 shorter events, 0.0 us)

commit v10 on v6

--- a/solution.py
+++ b/solution.py
@@ -528,6 +528,8 @@
         sums = sums + dot_of(hidden_rows[away, span(c)], value_rows[span(c), :], 1, 0)
     partial[:, half:] = sums
     swaps.append(swap(partial.at[:, pl.ds(half, half)], peer_partial.at[:, pl.ds(half, half)], 2))
+    for item in pieces:
+        spread(*item)
     mine_total = jnp.zeros((local, LANES), jnp.float32)
     key_sums = jnp.zeros((local, half), jnp.float32)
     value_sums = jnp.zeros((local, half), jnp.float32)
@@ -537,8 +539,6 @@
         key_sums = key_sums + dot_of(scaled, key_rows[span(c), :], 1, 0)
         value_sums = value_sums + dot_of(scaled, value_rows[span(c), :], 1, 0)
     own_squares = across(mine_total)
-    for item in pieces:
-        spread(*item)
 
     swaps[0].wait()
     eighths = jnp.full((SUBLANES, LANES), 1.0 / SUBLANES, jnp.float32)
@@ -564,6 +564,9 @@
     for turn in range(len(joint) + 2):
         if turn < len(joint):
             spread(*joint[turn])
+        if turn == 0:
+            for item in pieces:
+                relay(*item)
         if 1 <= turn < len(joint) + 1:
             relay(*joint[turn - 1])
         if turn == len(joint) + 1:
@@ -575,9 +578,6 @@
         if turn >= 2:
             finish(*joint[turn - 2])
         if turn == 1:
-            for item in pieces:
-                relay(*item)
-        if turn == 2:
             for item in pieces:
                 finish(*item)
         if turn == 3:

time: 75.9 us -> 74.3 us (0.979)
  Pallas kernels: 74.6 us -> 73 us
    pallas_call x1, Pallas kernels: 46.9 us -> 45.3 us  [collect(): pl.pallas_call(functools.partial(collect_kernel, heads), out_shape=(jax.S...]
where the time goes in v10:
time: 74.3 us; the launch traced here: 74.1 us
  Pallas kernels  73 us (98%)
  other arithmetic  1.08 us (1%)
    pallas_call x1, Pallas kernels, collect(): pl.pallas_call(functools.partial(collect_kernel, heads), out_shape=(jax.S...  45.3 us
    pallas_call x1, Pallas kernels, iterate(): pl.pallas_call(kernel, out_shape=jax.ShapeDtypeStruct((own.shape[1], rank...  27.7 us

profile of v10, /device:TPU:0, one launch (start us, length us, event | category | flops | bytes accessed | tf_op | source)
XLA Modules:
  0.0 74.1 jit_solution(17515612140362222938)
XLA Ops:
  0.0 0.7 convert_bitcast_fusion
  0.7 0.3 fusion
  1.0 0.1 pad_maximum_fusion
  1.1 45.3 %shard_map.64 = (bf16[1024,1024]{1,0:T(8,128)(2,1)S(1)}, bf16[1024,1024]{1,0:T(8,128)(2,1)S(1)}, f32[256,1024]{1,0:T(8,128)S(1)}, bf16[1024,512]{1,0:T(8,128)(2,1)S(1)}) custom-call(bf16[256,8192]{1,0:T(8,128)(2,1)} %bitcast.4, f32[1,8192]{1,0:T(1,128)} %bitcast.5, bf16[8192,256]{1,0:T(8,128)(2,1)} %key_ref.1, bf16[8192,256]{1,0:T(8,128)(2,1)} %value_ref.1, ...), custom_call_target="tpu_custom_call" | custom-call | tf_op jit(solution)/shard_map/pallas_call | solution.py:607
  46.4 27.7 %shard_map.65 = f32[512,256]{1,0:T(8,128)} custom-call(bf16[1024,1024]{1,0:T(8,128)(2,1)S(1)} %get-tuple-element.9.refs_0_, bf16[1024,1024]{1,0:T(8,128)(2,1)S(1)} %get-tuple-element.10.refs_1_, f32[256,1024]{1,0:T(8,128)S(1)} %get-tuple-element.11.refs_2_, bf16[1024,512]{1,0:T(8,128)(2,1)S(1)} %get-tuple-element.12.refs_3_), custom_call_target="tpu_custom_call" | custom-call | tf_op jit(solution)/shard_map/pallas_call | solution.py:264
  (1 shorter events, 0.0 us)

commit v11 on v10

--- a/solution.py
+++ b/solution.py
@@ -375,7 +375,7 @@
         load.wait()
         issue()
 
-    for _ in range(4):
+    for _ in range(6):
         issue()
 
     barrier = pltpu.get_barrier_semaphore()

time: 74.3 us -> 74.2 us (level)
  no operation moved by 1% of the time
where the time goes in v11:
time: 74.2 us; the launch traced here: 74.1 us
  Pallas kernels  73 us (98%)
  other arithmetic  1.08 us (1%)
    pallas_call x1, Pallas kernels, collect(): pl.pallas_call(functools.partial(collect_kernel, heads), out_shape=(jax.S...  45.3 us
    pallas_call x1, Pallas kernels, iterate(): pl.pallas_call(kernel, out_shape=jax.ShapeDtypeStruct((own.shape[1], rank...  27.7 us

profile of v11, /device:TPU:0, one launch (start us, length us, event | category | flops | bytes accessed | tf_op | source)
XLA Modules:
  0.0 74.1 jit_solution(3256023104442060929)
XLA Ops:
  0.0 0.7 convert_bitcast_fusion
  0.7 0.3 fusion
  1.0 0.1 pad_maximum_fusion
  1.1 45.3 %shard_map.64 = (bf16[1024,1024]{1,0:T(8,128)(2,1)S(1)}, bf16[1024,1024]{1,0:T(8,128)(2,1)S(1)}, f32[256,1024]{1,0:T(8,128)S(1)}, bf16[1024,512]{1,0:T(8,128)(2,1)S(1)}) custom-call(bf16[256,8192]{1,0:T(8,128)(2,1)} %bitcast.4, f32[1,8192]{1,0:T(1,128)} %bitcast.5, bf16[8192,256]{1,0:T(8,128)(2,1)} %key_ref.1, bf16[8192,256]{1,0:T(8,128)(2,1)} %value_ref.1, ...), custom_call_target="tpu_custom_call" | custom-call | tf_op jit(solution)/shard_map/pallas_call | solution.py:607
  46.4 27.7 %shard_map.65 = f32[512,256]{1,0:T(8,128)} custom-call(bf16[1024,1024]{1,0:T(8,128)(2,1)S(1)} %get-tuple-element.9.refs_0_, bf16[1024,1024]{1,0:T(8,128)(2,1)S(1)} %get-tuple-element.10.refs_1_, f32[256,1024]{1,0:T(8,128)S(1)} %get-tuple-element.11.refs_2_, bf16[1024,512]{1,0:T(8,128)(2,1)S(1)} %get-tuple-element.12.refs_3_), custom_call_target="tpu_custom_call" | custom-call | tf_op jit(solution)/shard_map/pallas_call | solution.py:264
  (1 shorter events, 0.0 us)
